TPU v7x, 512 devices: a whole 4x8x8 slice. The times are simulated.
512 devices in a mesh: dp: 64 (over y, x, core), mp: 8 (over z).
Axes of the slice: x: 4, y: 8, z: 8, core: 2. Of those that a mesh axis runs over, the one named last changes fastest.
Arguments:
- tokens: bfloat16 [65536, 2048], P('dp', 'mp'), may hold values from -6 to 6
- q_weight: bfloat16 [2048, 2048], P(None, 'mp'), may hold values from -0.125 to 0.125
- snippet_keys: bfloat16 [2048, 16, 2048], P('dp', None, 'mp'), may hold values from -500 to 500
- snippet_values: bfloat16 [2048, 16, 2048], P('dp', None, 'mp'), may hold values from -6 to 6
- out_cotangent: bfloat16 [65536, 2048], P('dp', 'mp'), may hold values from -6 to 6
- neighbour_ids: int32 [1024, 2], P('dp'), may hold values from 0 to 2047, as said below
- snippet_slot: int32 [2048], replicated, may hold values from 0 to 2047, as said below
Outputs:
- attended: bfloat16 [65536, 2048], P('dp', 'mp')
- input_grad: bfloat16 [65536, 2048], P('dp', 'mp')
- key_grad: float32 [2048, 16, 2048], P('dp', None, 'mp')
- value_grad: float32 [2048, 16, 2048], P('dp', None, 'mp')
Inputs may be any that keep to these rules, and one draw needn't show every extreme that they name: A permutation: snippet s lies at global row snippet_slot[s] of snippet_keys and snippet_values, that is on dp index snippet_slot[s] // 32. `neighbour_ids`: the 32 neighbours named by the spans of one dp index are distinct snippets; at most 1 of them are stored on any one dp index, and exactly 1 on some.
All inputs are finite; a program needn't handle non-finite values.
Results may differ from a plain program's by a relative error of at most 0.022.
The roundings to bfloat16 on the way count: a program that leaves them out, or rounds other values in their place, can miss the bound.
Values may be sent and summed in bfloat16 or wider, within the bound.
No kernel may reach another device: no remote copies, remote signals or barrier semaphores. Data moves between devices by JAX's collectives and lax.ppermute only.
A program may use at most 64 MiB of HBM per device.

v0:
```python
import math

import jax
import jax.numpy as jnp
from jax import lax
from jax.sharding import PartitionSpec as P

DH = 128
SPAN = 64
NEIGH = 2


def build_requests(id_block, slot_table, snip_count, dp_count, cap_count):
    flat_ids = id_block.reshape(-1)
    lookup = flat_ids[:, None] == jnp.arange(slot_table.shape[0], dtype=jnp.int32)[None, :]
    slots_used = jnp.sum(jnp.where(lookup, slot_table[None, :], 0), axis=1)
    owners = slots_used // snip_count
    row_ids = slots_used % snip_count
    pick_index = jnp.arange(flat_ids.shape[0], dtype=jnp.int32)
    earlier = (owners[:, None] == owners[None, :]) & (pick_index[:, None] > pick_index[None, :])
    ranks = jnp.sum(earlier.astype(jnp.int32), axis=1)
    positions = owners * cap_count + ranks
    slot_range = jnp.arange(dp_count * cap_count, dtype=jnp.int32)
    buffer = jnp.sum(
        jnp.where(positions[:, None] == slot_range[None, :], row_ids[:, None] + 1, 0), axis=0
    )
    return (buffer.reshape(dp_count, cap_count), positions)


def shift_into(matrix, head_count):
    padding = jnp.zeros((SPAN - 1, matrix.shape[1]), matrix.dtype)
    moved = jnp.concatenate([matrix[SPAN - 1 :], padding], axis=0)
    return moved.reshape(matrix.shape[0] // SPAN, SPAN, head_count, DH)


def shift_back(blocks):
    seq_len = blocks.shape[0] * blocks.shape[1]
    flat_rows = blocks.reshape(seq_len, blocks.shape[2] * blocks.shape[3])
    padding = jnp.zeros((SPAN - 1, flat_rows.shape[1]), blocks.dtype)
    return jnp.concatenate([padding, flat_rows[: seq_len - SPAN + 1]], axis=0)


def body(
    tokens, q_weight, snippet_keys, snippet_values, out_cotangent, neighbour_ids, snippet_slot
):
    dp_count = lax.axis_size("dp")
    seq_len = tokens.shape[0]
    local_width = q_weight.shape[1]
    head_count = local_width // DH
    snip_count = snippet_keys.shape[0]
    nei_tokens = snippet_keys.shape[1]
    span_count = seq_len // SPAN
    pick_total = span_count * NEIGH
    cap_count = (pick_total + dp_count - 1) // dp_count
    slot_count = cap_count * dp_count
    scaling = 1.0 / math.sqrt(DH)
    queries = jnp.dot(
        lax.all_gather(tokens, "mp", axis=1, tiled=True),
        q_weight,
        preferred_element_type=jnp.float32,
    ).astype(jnp.bfloat16)
    own_buffer, positions = build_requests(
        neighbour_ids, snippet_slot, snip_count, dp_count, cap_count
    )
    incoming = lax.all_to_all(own_buffer, "dp", split_axis=0, concat_axis=0, tiled=True)
    wanted = incoming.reshape(-1)
    is_valid = (wanted > 0)[:, None, None]
    row_index = jnp.maximum(wanted - 1, 0)
    send_keys = jnp.where(is_valid, snippet_keys[row_index], jnp.zeros((), jnp.bfloat16))
    send_values = jnp.where(is_valid, snippet_values[row_index], jnp.zeros((), jnp.bfloat16))
    got_keys, got_values = (
        lax.all_to_all(send_keys, "dp", split_axis=0, concat_axis=0, tiled=True),
        lax.all_to_all(send_values, "dp", split_axis=0, concat_axis=0, tiled=True),
    )
    span_keys = got_keys[positions].reshape(span_count, NEIGH * nei_tokens, head_count, DH)
    span_values = got_values[positions].reshape(span_count, NEIGH * nei_tokens, head_count, DH)
    shifted_q = shift_into(queries, head_count)
    grad_rows = shift_into(out_cotangent, head_count)
    scores = (
        jnp.einsum("cqhd,ckhd->chqk", shifted_q, span_keys, preferred_element_type=jnp.float32)
        * scaling
    )
    row_max = jnp.max(scores, axis=-1, keepdims=True)
    shifted_exp = jnp.exp(scores - row_max)
    weights = shifted_exp / jnp.sum(shifted_exp, axis=-1, keepdims=True)
    bf_weights = weights.astype(jnp.bfloat16)
    attended = shift_back(
        jnp.einsum(
            "chqk,ckhd->cqhd", bf_weights, span_values, preferred_element_type=jnp.float32
        ).astype(jnp.bfloat16)
    )
    prob_grad = jnp.einsum(
        "cqhd,ckhd->chqk", grad_rows, span_values, preferred_element_type=jnp.float32
    )
    row_delta = jnp.sum(weights * prob_grad, axis=-1, keepdims=True)
    score_grad = (weights * (prob_grad - row_delta)).astype(jnp.bfloat16)
    query_grads = shift_back(
        (
            jnp.einsum("chqk,ckhd->cqhd", score_grad, span_keys, preferred_element_type=jnp.float32)
            * scaling
        ).astype(jnp.bfloat16)
    )
    key_use = (
        jnp.einsum("chqk,cqhd->ckhd", score_grad, shifted_q, preferred_element_type=jnp.float32)
        * scaling
    )
    value_use = jnp.einsum(
        "chqk,cqhd->ckhd", bf_weights, grad_rows, preferred_element_type=jnp.float32
    )
    key_send = (
        jnp.zeros((slot_count, nei_tokens, local_width), jnp.float32)
        .at[positions]
        .set(key_use.reshape(pick_total, nei_tokens, local_width))
    )
    value_send = (
        jnp.zeros((slot_count, nei_tokens, local_width), jnp.float32)
        .at[positions]
        .set(value_use.reshape(pick_total, nei_tokens, local_width))
    )
    owner_map = (wanted[None, :] == (jnp.arange(snip_count, dtype=jnp.int32) + 1)[:, None]).astype(
        jnp.float32
    )
    back_keys, back_values = (
        lax.all_to_all(key_send, "dp", split_axis=0, concat_axis=0, tiled=True),
        lax.all_to_all(value_send, "dp", split_axis=0, concat_axis=0, tiled=True),
    )
    key_grad = jnp.dot(
        owner_map,
        back_keys.reshape(slot_count, nei_tokens * local_width),
        preferred_element_type=jnp.float32,
        precision=lax.Precision.HIGHEST,
    ).reshape(snip_count, nei_tokens, local_width)
    value_grad = jnp.dot(
        owner_map,
        back_values.reshape(slot_count, nei_tokens * local_width),
        preferred_element_type=jnp.float32,
        precision=lax.Precision.HIGHEST,
    ).reshape(snip_count, nei_tokens, local_width)
    grad_terms = lax.dot_general(
        query_grads, q_weight, (((1,), (1,)), ((), ())), preferred_element_type=jnp.float32
    )
    input_grad = lax.psum_scatter(
        grad_terms.astype(jnp.bfloat16), "mp", scatter_dimension=1, tiled=True
    )
    return (attended, input_grad, key_grad, value_grad)


def solution(mesh):
    return jax.shard_map(
        body,
        mesh=mesh,
        in_specs=(
            P("dp", "mp"),
            P(None, "mp"),
            P("dp", None, "mp"),
            P("dp", None, "mp"),
            P("dp", "mp"),
            P("dp", None),
            P(),
        ),
        out_specs=(P("dp", "mp"), P("dp", "mp"), P("dp", None, "mp"), P("dp", None, "mp")),
        check_vma=False,
    )
```

profile of v0, /device:TPU:1, one launch (start us, length us, event | category | flops | bytes accessed | tf_op | source)
XLA Modules:
  0.0 179.8 jit_solution(8224479871887196211)
XLA Ops:
  10.1 20.8 %all_to_all.29 = s32[64,1,1]{2,1,0:T(1,128)S(1)} all-to-all(s32[64,1,1]{2,1,0:T(1,128)S(1)} %copy.74), channel_id=1, replica_groups=mesh['dp'=64,'mp'=8] {'dp'}, dimensions={0} | all-to-all | bytes 512 | tf_op jit(solution)/shard_map/all_to_all | solution.py:65
  30.9 2.4 %fusion.37 = (s32[64]{0:T(128)S(1)}, s32[64]{0:T(128)S(1)}) fusion(s32[64,1,1]{2,1,0:T(1,128)S(1)} %all_to_all.29), kind=kLoop, calls=%fused_computation.80 | loop fusion | flops 128 | bytes 768 | tf_op jit(solution)/shard_map/all_to_all | solution.py:65
  33.3 1.6 gather_fusion.2
  34.8 1.5 gather_fusion
  36.4 1.2 compare_reduce_fusion
  38.5 21.7 %all_to_all.30 = bf16[64,16,256]{2,1,0:T(8,128)(2,1)S(1)} all-to-all(bf16[64,16,256]{2,1,0:T(8,128)(2,1)S(1)} %get-tuple-element.26), channel_id=1, replica_groups=mesh['dp'=64,'mp'=8] {'dp'}, dimensions={0} | all-to-all | bytes 1048576 | tf_op jit(solution)/shard_map/all_to_all | solution.py:72
  60.3 5.7 %all-to-all-start.1 = ((bf16[64,16,256]{2,1,0:T(8,128)(2,1)}), bf16[64,16,256]{2,1,0:T(8,128)(2,1)S(1)}, u32[]{:S(2)}, u32[]{:S(2)}) async-start(bf16[64,16,256]{2,1,0:T(8,128)(2,1)} %get-tuple-element.27), calls=%async_computation.1 | async-start | bytes 1048576 | tf_op jit(solution)/shard_map/all_to_all | solution.py:73
  67.2 16.5 %all-to-all-done.1 = bf16[64,16,256]{2,1,0:T(8,128)(2,1)S(1)} async-done(((bf16[64,16,256]{2,1,0:T(8,128)(2,1)}), bf16[64,16,256]{2,1,0:T(8,128)(2,1)S(1)}, u32[]{:S(2)}, u32[]{:S(2)}) %all-to-all-start.1) | async-done | bytes 524320 | tf_op jit(solution)/shard_map/all_to_all | solution.py:73
  84.4 3.4 %fusion.39 = bf16[1024,256]{1,0:T(8,128)(2,1)S(1)} fusion(bf16[1024,2048]{1,0:T(8,128)(2,1)} %all-gather.2.cloned.1.call-done, bf16[2048,256]{1,0:T(8,128)(2,1)S(1)} %copy-done), kind=kOutput, calls=%fused_computation.84 | convolution fusion | flops 1073741824 | bytes 5767168 | tf_op jit(solution)/shard_map/dot_general | solution.py:57
  88.5 1.3 fusion.38
  91.4 3.2 %convolution_convert_fusion = bf16[1024,2048]{1,0:T(8,128)(2,1)} fusion(bf16[2048,256]{1,0:T(8,128)(2,1)S(1)} %copy-done, bf16[961,256]{1,0:T(8,128)(2,1)S(1)} %slice.26), kind=kOutput, calls=%fused_computation.7 | convolution fusion | flops 1075838976 | bytes 5734912 | tf_op jit(solution)/shard_map/dot_general | solution.py:139
  95.8 1.1 broadcast.223.clone
  96.9 4.3 %scatter_fusion = f32[64,16,256]{2,1,0:T(8,128)} fusion(f32[64,16,256]{2,1,0:T(8,128)} %broadcast.223.clone, s32[32]{0:T(128)S(1)} %fusion.35, f32[32,16,256]{2,1,0:T(8,128)S(1)} %reshape.225), kind=kCustom, calls=%fused_computation.4 | custom fusion | bytes 1572992 | tf_op jit(solution)/shard_map/scatter | solution.py:113
  101.2 7.1 %all-to-all-start.3 = ((f32[64,16,256]{2,1,0:T(8,128)}), f32[64,16,256]{2,1,0:T(8,128)S(1)}, u32[]{:S(2)}, u32[]{:S(2)}) async-start(f32[64,16,256]{2,1,0:T(8,128)} %scatter_fusion), calls=%async_computation.4 | async-start | bytes 2097152 | tf_op jit(solution)/shard_map/all_to_all | solution.py:124
  109.5 1.4 copy.87
  111.3 1.1 broadcast.223.clone.1
  112.5 4.4 %scatter_fusion.1 = f32[64,16,256]{2,1,0:T(8,128)} fusion(f32[64,16,256]{2,1,0:T(8,128)} %broadcast.223.clone.1, s32[32]{0:T(128)S(1)} %fusion.35, f32[32,16,256]{2,1,0:T(8,128)S(1)} %reshape.233), kind=kCustom, calls=%fused_computation.5 | custom fusion | bytes 1572992 | tf_op jit(solution)/shard_map/scatter | solution.py:118
  116.8 19.5 %all-to-all-done.3 = f32[64,16,256]{2,1,0:T(8,128)S(1)} async-done(((f32[64,16,256]{2,1,0:T(8,128)}), f32[64,16,256]{2,1,0:T(8,128)S(1)}, u32[]{:S(2)}, u32[]{:S(2)}) %all-to-all-start.3) | async-done | bytes 1048608 | tf_op jit(solution)/shard_map/all_to_all | solution.py:124
  136.3 6.5 %all-to-all-start.4 = ((f32[64,16,256]{2,1,0:T(8,128)}), f32[64,16,256]{2,1,0:T(8,128)S(1)}, u32[]{:S(2)}, u32[]{:S(2)}) async-start(f32[64,16,256]{2,1,0:T(8,128)} %scatter_fusion.1), calls=%async_computation.5 | async-start | bytes 2097152 | tf_op jit(solution)/shard_map/all_to_all | solution.py:125
  142.8 2.4 %fusion.4 = bf16[16,64,2,128]{3,1,2,0:T(8,128)(2,1)} fusion(bf16[16,32,2,128]{3,2,1,0:T(2,128)(2,1)S(1)} %reshape.179, f32[16,2,64]{2,1,0:T(2,128)S(1)} %get-tuple-element.30, f32[16,2,64,32]{2,3,1,0:T(8,128)} %copy-done.1), kind=kOutput, calls=%fused_computation.13 | convolution fusion | flops 17238048 | bytes 1056768 | tf_op jit(solution)/shard_map/chqk,ckhd->cqhd/dot_general | solution.py:88
  145.2 1.6 copy.78
  147.8 1.1 fusion.10
  150.1 20.7 %all-to-all-done.4 = f32[64,16,256]{2,1,0:T(8,128)S(1)} async-done(((f32[64,16,256]{2,1,0:T(8,128)}), f32[64,16,256]{2,1,0:T(8,128)S(1)}, u32[]{:S(2)}, u32[]{:S(2)}) %all-to-all-start.4) | async-done | bytes 1048608 | tf_op jit(solution)/shard_map/all_to_all | solution.py:125
  170.8 1.1 fusion.7
  (52 shorter events, 13.7 us)
Async XLA Ops:
  7.2 77.2 %copy-start = (bf16[2048,256]{1,0:T(8,128)(2,1)S(1)}, bf16[2048,256]{1,0:T(8,128)(2,1)}, u32[]{:S(2)}) copy-start(bf16[2048,256]{1,0:T(8,128)(2,1)} %param.8) | copy-start | bytes 3145732
  7.2 59.1 %copy-start.2 = (bf16[1024,256]{1,0:T(8,128)(2,1)S(1)}, bf16[1024,256]{1,0:T(8,128)(2,1)}, u32[]{:S(2)}) copy-start(bf16[1024,256]{1,0:T(8,128)(2,1)} %param.11) | copy-start | bytes 1572868
  7.2 77.2 %all-gather.2.cloned.1.call-start = ((), (), s32[]{:S(2)}) async-start(), calls=%async_computation.6 | async-start | bytes 4718592 | tf_op jit(solution)/shard_map/all_gather | solution.py:58
  60.3 23.4 %all-to-all-start.1 = ((bf16[64,16,256]{2,1,0:T(8,128)(2,1)}), bf16[64,16,256]{2,1,0:T(8,128)(2,1)S(1)}, u32[]{:S(2)}, u32[]{:S(2)}) async-start(bf16[64,16,256]{2,1,0:T(8,128)(2,1)} %get-tuple-element.27), calls=%async_computation.1 | async-start | bytes 1048576 | tf_op jit(solution)/shard_map/all_to_all | solution.py:73
  66.0 107.0 %reduce-scatter.2.cloned.1.call-start = ((), (), s32[]{:S(2)}) async-start(), calls=%async_computation.7 | async-start | bytes 4718592 | tf_op jit(solution)/shard_map/reduce_scatter | solution.py:142
  88.5 19.8 %copy-start.1 = (f32[16,2,64,32]{2,3,1,0:T(8,128)}, f32[16,2,64,32]{2,3,1,0:T(8,128)S(1)}, u32[]{:S(2)}) copy-start(f32[16,2,64,32]{2,3,1,0:T(8,128)S(1)} %convolution_multiply_fusion.2) | copy-start | bytes 786436
  101.2 35.1 %all-to-all-start.3 = ((f32[64,16,256]{2,1,0:T(8,128)}), f32[64,16,256]{2,1,0:T(8,128)S(1)}, u32[]{:S(2)}, u32[]{:S(2)}) async-start(f32[64,16,256]{2,1,0:T(8,128)} %scatter_fusion), calls=%async_computation.4 | async-start | bytes 2097152 | tf_op jit(solution)/shard_map/all_to_all | solution.py:124
  136.3 34.5 %all-to-all-start.4 = ((f32[64,16,256]{2,1,0:T(8,128)}), f32[64,16,256]{2,1,0:T(8,128)S(1)}, u32[]{:S(2)}, u32[]{:S(2)}) async-start(f32[64,16,256]{2,1,0:T(8,128)} %scatter_fusion.1), calls=%async_computation.5 | async-start | bytes 2097152 | tf_op jit(solution)/shard_map/all_to_all | solution.py:125
Sparse Core Ops, SparseCore 0:
  10.0 68.8 all-gather.1
  94.8 58.3 reduce-scatter.1
where the time goes:
time: 181 us; the launch traced here: 180 us
  waiting for transfers between devices  57.4 us (32%)
  blocking collectives  42.5 us (23%)
  local copies, waits for them, and re-layouts  25 us (14%)
  starting transfers between devices  19.5 us (11%)
  between operations  14.4 us (8%)
  matrix products  13.8 us (8%)
  other arithmetic  7.21 us (4%)
    all_to_all x1, blocking collectives, body(): lax.all_to_all(send_keys, 'dp', split_axis=0, concat_axis=0, tiled=True)  21.7 us
    all_to_all x1, blocking collectives, body(): lax.all_to_all(own_buffer, 'dp', split_axis=0, concat_axis=0, tiled=True)  20.8 us
    all_to_all x1, waiting for transfers between devices, body(): lax.all_to_all(value_send, 'dp', split_axis=0, concat_axis=0, tiled=True)  20.7 us
    all_to_all x1, waiting for transfers between devices, body(): lax.all_to_all(key_send, 'dp', split_axis=0, concat_axis=0, tiled=True)  19.5 us
    all_to_all x1, waiting for transfers between devices, body(): lax.all_to_all(send_values, 'dp', split_axis=0, concat_axis=0, tiled=True)  16.5 us
    all_to_all x1, starting transfers between devices, body(): lax.all_to_all(key_send, 'dp', split_axis=0, concat_axis=0, tiled=True)  7.09 us
    all_to_all x1, starting transfers between devices, body(): lax.all_to_all(value_send, 'dp', split_axis=0, concat_axis=0, tiled=True)  6.47 us
    all_to_all x1, starting transfers between devices, body(): lax.all_to_all(send_values, 'dp', split_axis=0, concat_axis=0, tiled=True)  5.72 us
  transfers between devices with their start and end apart: 5, of which 3 were waited for; matrix products, arithmetic and copies ran while one was open for 20% of the time, Pallas kernels for 0%

commit v1 on v0

v1 whole, which is shorter than its diff:
```python
import math

import jax
import jax.numpy as jnp
from jax import lax
from jax.experimental import pallas as pl
from jax.experimental.pallas import tpu as pltpu
from jax.sharding import PartitionSpec as P

DH = 128
SPAN = 64
NEIGH = 2
TILE = 2 * SPAN
BLOCK = 2 * TILE
LANES = 128
F32 = jnp.float32
BF16 = jnp.bfloat16

VMEM = pl.BlockSpec(memory_space=pltpu.MemorySpace.VMEM)
SMEM = pl.BlockSpec(memory_space=pltpu.MemorySpace.SMEM)
HBM = pl.BlockSpec(memory_space=pltpu.MemorySpace.HBM)


def dot_nt(a, b):
    return lax.dot_general(a, b, (((1,), (1,)), ((), ())), preferred_element_type=F32)


def dot_tn(a, b):
    return lax.dot_general(a, b, (((0,), (0,)), ((), ())), preferred_element_type=F32)


def request_rows(ids, slot_table, snip_count, dp_count):
    spans = ids.shape[1]

    def kernel(ids_ref, slot_ref, req_ref, own_ref):
        def clear(i, c):
            req_ref[i, 0, 0] = 0
            return c

        lax.fori_loop(0, dp_count, clear, 0)

        def step(i, c):
            for n in range(NEIGH):
                slot = slot_ref[ids_ref[n, i]]
                owner = lax.div(slot, snip_count)
                req_ref[owner, 0, 0] = slot - owner * snip_count + 1
                own_ref[i * NEIGH + n] = owner
            return c

        lax.fori_loop(0, spans, step, 0)

    return pl.pallas_call(
        kernel,
        out_shape=(
            jax.ShapeDtypeStruct((dp_count, 1, LANES), jnp.int32),
            jax.ShapeDtypeStruct((spans * NEIGH,), jnp.int32),
        ),
        in_specs=[SMEM, SMEM],
        out_specs=(SMEM, SMEM),
        name="request_rows",
    )(ids, slot_table)


def pick_rows(wanted, keys, values):
    dp_count = wanted.shape[0]
    _, nei, width = keys.shape

    def kernel(want_ref, key_ref, value_ref, out_ref):
        def step(i, c):
            row = jnp.maximum(want_ref[i, 0, 0] - 1, 0)
            out_ref[i, :, :width] = key_ref[row]
            out_ref[i, :, width:] = value_ref[row]
            return c

        lax.fori_loop(0, dp_count, step, 0, unroll=4)

    return pl.pallas_call(
        kernel,
        out_shape=jax.ShapeDtypeStruct((dp_count, nei, 2 * width), keys.dtype),
        in_specs=[SMEM, VMEM, VMEM],
        out_specs=VMEM,
        name="pick_rows",
    )(wanted, keys, values)


def sum_uses(wanted, back, snip_count):
    dp_count, nei, twice = back.shape
    width = twice // 2

    def kernel(want_ref, back_ref, key_ref, value_ref):
        key_ref[...] = jnp.zeros_like(key_ref)
        value_ref[...] = jnp.zeros_like(value_ref)

        def step(i, c):
            want = want_ref[i, 0, 0]

            @pl.when(want > 0)
            def _():
                row = jnp.maximum(want - 1, 0)
                key_ref[row] += back_ref[i, :, :width].astype(F32)
                value_ref[row] += back_ref[i, :, width:].astype(F32)

            return c

        lax.fori_loop(0, dp_count, step, 0)

    out = jax.ShapeDtypeStruct((snip_count, nei, width), F32)
    return pl.pallas_call(
        kernel,
        out_shape=(out, out),
        in_specs=[SMEM, VMEM],
        out_specs=(VMEM, VMEM),
        name="sum_uses",
    )(wanted, back)


def attend(owners, tokens, q_weight, cotangent, got):
    seq_len, width = cotangent.shape
    mp_count = tokens.shape[0]
    dp_count, nei, _ = got.shape
    heads = width // DH
    picks = owners.shape[0]
    span_keys = NEIGH * nei
    tile_keys = 3 * span_keys
    blocks = seq_len // BLOCK
    scaling = 1.0 / math.sqrt(DH)

    def kernel(
        own_ref, tok_hbm, w_ref, cot_hbm, got_ref, att_ref, term_hbm, use_ref,
        tok_ref, cot_ref, term_ref, q_ref, qg_ref, k_ref, v_ref, ku_ref, vu_ref, in_sem, cot_sem, out_sem,
    ):
        def load(b):
            rows = slice(b * BLOCK, (b + 1) * BLOCK)
            return pltpu.make_async_copy(tok_hbm.at[:, rows, :], tok_ref.at[:, rows, :], in_sem.at[b])

        def store(b):
            rows = slice(b * BLOCK, (b + 1) * BLOCK)
            return pltpu.make_async_copy(term_ref.at[rows, :], term_hbm.at[rows, :], out_sem.at[b])

        load(0).start()
        load_cot = pltpu.make_async_copy(cot_hbm, cot_ref, cot_sem)
        load_cot.start()
        for b in range(1, blocks):
            load(b).start()
        k_ref[:span_keys, :] = jnp.zeros((span_keys, width), BF16)
        v_ref[:span_keys, :] = jnp.zeros((span_keys, width), BF16)
        for n in range(picks):
            at = span_keys + n * nei
            k_ref[at : at + nei, :] = got_ref[own_ref[n], :, :width]
            v_ref[at : at + nei, :] = got_ref[own_ref[n], :, width:]
        use_ref[...] = jnp.zeros_like(use_ref)
        key_at = lax.broadcasted_iota(jnp.int32, (tile_keys, TILE), 0) // span_keys
        span_of = (lax.broadcasted_iota(jnp.int32, (tile_keys, TILE), 1) + 1) // SPAN
        inner = key_at == span_of
        first_tile = inner & (key_at > 0)

        def one_tile(t):
            mask = inner if t else first_tile
            rows = slice(t * TILE, (t + 1) * TILE)
            start = t * NEIGH * span_keys
            keys_at = slice(start, start + tile_keys)
            for h in range(heads):
                cols = slice(h * DH, (h + 1) * DH)
                q = q_ref[rows, cols]
                cot = cot_ref[rows, cols]
                k = k_ref[keys_at, cols]
                v = v_ref[keys_at, cols]
                scores = jnp.where(mask, dot_nt(k, q) * scaling, -jnp.inf)
                top = jnp.max(scores, axis=0, keepdims=True)
                top = jnp.where(top == -jnp.inf, 0.0, top)
                grown = jnp.exp(scores - top)
                total = jnp.sum(grown, axis=0, keepdims=True)
                weights = grown * (1.0 / jnp.where(total > 0.0, total, 1.0))
                bf_weights = weights.astype(BF16)
                prob_grad = dot_nt(v, cot)
                row_delta = jnp.sum(weights * prob_grad, axis=0, keepdims=True)
                score_grad = (weights * (prob_grad - row_delta)).astype(BF16)
                att_ref[rows, cols] = dot_tn(bf_weights, v).astype(BF16)
                qg_ref[rows, cols] = (dot_tn(score_grad, k) * scaling).astype(BF16)
                key_use = jnp.dot(score_grad, q, preferred_element_type=F32)
                value_use = jnp.dot(bf_weights, cot, preferred_element_type=F32)
                mid, end = start + span_keys, start + tile_keys
                if t == 0:
                    ku_ref[start:mid, cols] = key_use[:span_keys]
                    vu_ref[start:mid, cols] = value_use[:span_keys]
                else:
                    ku_ref[start:mid, cols] += key_use[:span_keys]
                    vu_ref[start:mid, cols] += value_use[:span_keys]
                ku_ref[mid:end, cols] = key_use[span_keys:]
                vu_ref[mid:end, cols] = value_use[span_keys:]

        for b in range(blocks):
            rows = slice(b * BLOCK, (b + 1) * BLOCK)
            load(b).wait()
            acc = None
            for j in range(mp_count):
                w = w_ref[j * width : (j + 1) * width, :]
                x = jnp.dot(tok_ref[j, rows, :], w, preferred_element_type=F32)
                acc = x if acc is None else acc + x
            q_ref[rows, :] = acc.astype(BF16)
            if b == 0:
                load_cot.wait()
            for t in range(b * BLOCK // TILE, (b + 1) * BLOCK // TILE):
                one_tile(t)
            qg = qg_ref[rows, :]
            for j in range(mp_count):
                at = slice(j * width, (j + 1) * width)
                term_ref[rows, at] = dot_nt(qg, w_ref[at, :]).astype(BF16)
            store(b).start()
        for n in range(picks):
            at = span_keys + n * nei
            use_ref[own_ref[n], :, :width] = (ku_ref[at : at + nei, :] * scaling).astype(BF16)
            use_ref[own_ref[n], :, width:] = vu_ref[at : at + nei, :].astype(BF16)
        for b in range(blocks):
            store(b).wait()

    padded = (seq_len // SPAN + 1) * span_keys
    return pl.pallas_call(
        kernel,
        out_shape=(
            jax.ShapeDtypeStruct((seq_len, width), BF16),
            jax.ShapeDtypeStruct((seq_len, mp_count * width), BF16),
            jax.ShapeDtypeStruct((dp_count, nei, 2 * width), BF16),
        ),
        in_specs=[SMEM, HBM, VMEM, HBM, VMEM],
        out_specs=(VMEM, HBM, VMEM),
        scratch_shapes=[
            pltpu.VMEM((mp_count, seq_len, width), BF16),
            pltpu.VMEM((seq_len, width), BF16),
            pltpu.VMEM((seq_len, mp_count * width), BF16),
            pltpu.VMEM((seq_len, width), BF16),
            pltpu.VMEM((seq_len, width), BF16),
            pltpu.VMEM((padded, width), BF16),
            pltpu.VMEM((padded, width), BF16),
            pltpu.VMEM((padded, width), F32),
            pltpu.VMEM((padded, width), F32),
            pltpu.SemaphoreType.DMA((blocks,)),
            pltpu.SemaphoreType.DMA(()),
            pltpu.SemaphoreType.DMA((blocks,)),
        ],
        compiler_params=pltpu.CompilerParams(vmem_limit_bytes=24 * 1024 * 1024),
        name="attend",
    )(owners, tokens, q_weight, cotangent, got)


def body(
    tokens, q_weight, snippet_keys, snippet_values, out_cotangent, neighbour_ids, snippet_slot
):
    dp_count = lax.axis_size("dp")
    snip_count = snippet_keys.shape[0]
    gathered = lax.all_gather(tokens, "mp", axis=0, tiled=False)
    request, owners = request_rows(neighbour_ids.T, snippet_slot, snip_count, dp_count)
    wanted = lax.all_to_all(request, "dp", split_axis=0, concat_axis=0, tiled=True)
    picked = pick_rows(wanted, snippet_keys, snippet_values)
    got = lax.all_to_all(picked, "dp", split_axis=0, concat_axis=0, tiled=True)
    attended, terms, uses = attend(owners, gathered, q_weight, out_cotangent, got)
    input_grad = lax.psum_scatter(terms, "mp", scatter_dimension=1, tiled=True)
    back = lax.all_to_all(uses, "dp", split_axis=0, concat_axis=0, tiled=True)
    key_grad, value_grad = sum_uses(wanted, back, snip_count)
    return (attended, input_grad, key_grad, value_grad)


def solution(mesh):
    return jax.shard_map(
        body,
        mesh=mesh,
        in_specs=(
            P("dp", "mp"),
            P(None, "mp"),
            P("dp", None, "mp"),
            P("dp", None, "mp"),
            P("dp", "mp"),
            P("dp", None),
            P(),
        ),
        out_specs=(P("dp", "mp"), P("dp", "mp"), P("dp", None, "mp"), P("dp", None, "mp")),
        check_vma=False,
    )
```

time: 181 us -> 156 us (0.86)
  blocking collectives: 42.5 us -> 92.2 us
  waiting for transfers between devices: 57.4 us -> 23.1 us
  Pallas kernels: 0 us -> 20.2 us
  starting transfers between devices: 19.5 us -> 0.08 us
  local copies, waits for them, and re-layouts: 25 us -> 5.84 us
  matrix products: 13.8 us -> 0 us
  other arithmetic: 7.21 us -> 0 us
    all_to_all x3 -> x0, waiting for transfers between devices: 56.7 us -> none  [the longest x1 20.7 us: body(): lax.all_to_all(value_send, 'dp', split_axis=0, concat_axis=0, tiled=True)]
    all_to_all x2 -> x3, blocking collectives: 42.5 us -> 92.2 us  [the longest x1 38.3 us: body(): back = lax.all_to_all(uses, 'dp', split_axis=0, concat_axis=0, tiled=True)]
    pallas_call x0 -> x4, Pallas kernels: none -> 20.2 us  [the longest x1 11.9 us: attend(): pl.pallas_call(kernel, out_shape=(jax.ShapeDtypeStruct((seq_len, width),...]
    all_to_all x3 -> x0, starting transfers between devices: 19.3 us -> none  [the longest x1 7.09 us: body(): lax.all_to_all(key_send, 'dp', split_axis=0, concat_axis=0, tiled=True)]
    reduce_scatter x1, waiting for transfers between devices: 0.01 us -> 15.3 us  [body(): input_grad = lax.psum_scatter(terms, 'mp', scatter_dimension=1, tiled=True)]
    dot_general x10 -> x0, matrix products: 13.8 us -> none  [the longest x1 3.43 us: body(): jnp.dot(lax.all_gather(tokens, 'mp', axis=1, tiled=True), q_weight, prefe...]
    scatter x2 -> x0, local copies, waits for them, and re-layouts: 8.71 us -> none  [the longest x1 4.37 us: body(): value_send = jnp.zeros((slot_count, nei_tokens, local_width), jnp.float32...]
    all_gather x1, waiting for transfers between devices: 0.02 us -> 7.05 us  [body(): gathered = lax.all_gather(tokens, 'mp', axis=0, tiled=False)]
  transfers between devices with their start and end apart: 5 -> 2, of which waited for: 3 -> 2; matrix products, arithmetic and copies ran while one was open for 20% -> 0% of each run, Pallas kernels for 0% -> 5%
where the time goes in v1:
time: 156 us; the launch traced here: 155 us
  blocking collectives  92.2 us (59%)
  waiting for transfers between devices  23.1 us (15%)
  Pallas kernels  20.2 us (13%)
  between operations  14.1 us (9%)
  local copies, waits for them, and re-layouts  5.84 us (4%)
    all_to_all x1, blocking collectives, body(): back = lax.all_to_all(uses, 'dp', split_axis=0, concat_axis=0, tiled=True)  38.3 us
    all_to_all x1, blocking collectives, body(): got = lax.all_to_all(picked, 'dp', split_axis=0, concat_axis=0, tiled=True)  32.8 us
    all_to_all x1, blocking collectives, body(): lax.all_to_all(request, 'dp', split_axis=0, concat_axis=0, tiled=True)  21.2 us
    reduce_scatter x1, waiting for transfers between devices, body(): input_grad = lax.psum_scatter(terms, 'mp', scatter_dimension=1, tiled=True)  15.3 us
    pallas_call x1, Pallas kernels, attend(): pl.pallas_call(kernel, out_shape=(jax.ShapeDtypeStruct((seq_len, width),...  11.9 us
    all_gather x1, waiting for transfers between devices, body(): gathered = lax.all_gather(tokens, 'mp', axis=0, tiled=False)  7.05 us
    unnamed x10, local copies, waits for them, and re-layouts  5.84 us
    pallas_call x1, Pallas kernels, sum_uses(): pl.pallas_call(kernel, out_shape=(out, out), in_specs=[SMEM, VMEM], out_s...  3.39 us
  transfers between devices with their start and end apart: 2, of which 2 were waited for; matrix products, arithmetic and copies ran while one was open for 0% of the time, Pallas kernels for 5%

profile of v1, /device:TPU:1, one launch (start us, length us, event | category | flops | bytes accessed | tf_op | source)
XLA Modules:
  0.0 155.5 jit_solution(8264026546254393599)
XLA Ops:
  7.2 0.0 copy-start.2
  7.2 0.0 all-gather.3.cloned.1.call-start
  7.2 0.7 all-gather.3.cloned.1.call-update
  7.9 0.0 reduce-scatter.2.cloned.1.call-start
  8.0 2.5 %request_rows.1 = (s32[64,1,128]{2,1,0:T(1,128)}, s32[32]{0:T(128)}) custom-call(s32[2,16]{1,0:T(2,128)} %bitcast.3, s32[2048]{0:T(1024)} %slot_ref.1), custom_call_target="tpu_custom_call" | custom-call | tf_op jit(solution)/shard_map/request_rows/pallas_call | solution.py:52
  10.5 21.2 %all_to_all.15.want_ref = s32[64,1,128]{2,1,0:T(1,128)} all-to-all(s32[64,1,128]{2,1,0:T(1,128)} %get-tuple-element.12), channel_id=1, replica_groups=mesh['dp'=64,'mp'=8] {'dp'}, dimensions={0} | all-to-all | bytes 65536 | tf_op jit(solution)/shard_map/all_to_all | solution.py:253
  31.7 2.4 %pick_rows.1 = bf16[64,16,512]{2,1,0:T(8,128)(2,1)} custom-call(s32[64,1,128]{2,1,0:T(1,128)} %all_to_all.15.want_ref, bf16[32,16,256]{2,1,0:T(8,128)(2,1)} %key_ref.1, bf16[32,16,256]{2,1,0:T(8,128)(2,1)} %value_ref.1), custom_call_target="tpu_custom_call" | custom-call | tf_op jit(solution)/shard_map/pick_rows/pallas_call | solution.py:77
  34.0 32.8 %all_to_all.16.got_ref = bf16[64,16,512]{2,1,0:T(8,128)(2,1)S(1)} all-to-all(bf16[64,16,512]{2,1,0:T(8,128)(2,1)} %pick_rows.1), channel_id=1, replica_groups=mesh['dp'=64,'mp'=8] {'dp'}, dimensions={0} | all-to-all | bytes 2097152 | tf_op jit(solution)/shard_map/all_to_all | solution.py:255
  66.8 7.0 %all-gather.3.cloned.1.call-done = bf16[8192,256]{1,0:T(8,128)(2,1)} async-done(((bf16[1024,256]{1,0:T(8,128)(2,1)}), bf16[8192,256]{1,0:T(8,128)(2,1)}) %all-gather.3.cloned.1.call-update) | async-done | bytes 4194320 | tf_op jit(solution)/shard_map/all_gather | solution.py:251
  73.9 0.0 copy-done.2
  73.9 0.0 copy-start
  73.9 2.2 %copy-done = bf16[8192,256]{1,0:T(8,128)(2,1)S(1)} copy-done((bf16[8192,256]{1,0:T(8,128)(2,1)S(1)}, bf16[8192,256]{1,0:T(8,128)(2,1)}, u32[]{:S(2)}) %copy-start) | copy-done | bytes 4194328
  76.1 0.0 copy-start.3
  76.1 1.0 copy-done.3
  77.1 0.0 copy-start.4
  77.1 0.7 copy-done.4
  77.8 11.9 %attend.1 = (bf16[1024,256]{1,0:T(8,128)(2,1)}, bf16[1024,2048]{1,0:T(8,128)(2,1)S(1)}, bf16[64,16,512]{2,1,0:T(8,128)(2,1)S(1)}) custom-call(s32[32]{0:T(128)S(1)} %copy-done.4, bf16[8,1024,256]{2,1,0:T(8,128)(2,1)S(1)} %bitcast.2, bf16[2048,256]{1,0:T(8,128)(2,1)S(1)} %copy-done.2, bf16[1024,256]{1,0:T(8,128)(2,1)S(1)} %copy-done.3, ...), custom_call_target="tpu_custom_call" | custom-call | tf_op jit(solution)/shard_map/attend/pallas_call | solution.py:218
  89.6 0.0 copy-start.1
  89.7 1.9 %copy-done.1 = bf16[1024,2048]{1,0:T(8,128)(2,1)} copy-done((bf16[1024,2048]{1,0:T(8,128)(2,1)}, bf16[1024,2048]{1,0:T(8,128)(2,1)S(1)}, u32[]{:S(2)}) %copy-start.1) | copy-done | bytes 4194328
  91.6 0.0 reduce-scatter.2.cloned.1.call-update
  91.6 38.3 %all_to_all.17.back_ref = bf16[64,16,512]{2,1,0:T(8,128)(2,1)} all-to-all(bf16[64,16,512]{2,1,0:T(8,128)(2,1)S(1)} %get-tuple-element.15), channel_id=1, replica_groups=mesh['dp'=64,'mp'=8] {'dp'}, dimensions={0} | all-to-all | bytes 2097152 | tf_op jit(solution)/shard_map/all_to_all | solution.py:258
  129.9 3.4 %sum_uses.1 = (f32[32,16,256]{2,1,0:T(8,128)}, f32[32,16,256]{2,1,0:T(8,128)}) custom-call(s32[64,1,128]{2,1,0:T(1,128)} %all_to_all.15.want_ref, bf16[64,16,512]{2,1,0:T(8,128)(2,1)} %all_to_all.17.back_ref), custom_call_target="tpu_custom_call" | custom-call | tf_op jit(solution)/shard_map/sum_uses/pallas_call | solution.py:108
  133.3 15.3 %reduce-scatter.2.cloned.1.call-done = bf16[1024,256]{1,0:T(8,128)(2,1)} async-done(((bf16[1024,2048]{1,0:T(8,128)(2,1)}), bf16[1024,256]{1,0:T(8,128)(2,1)}) %reduce-scatter.2.cloned.1.call-update) | async-done | bytes 524304 | tf_op jit(solution)/shard_map/reduce_scatter | solution.py:257
Async XLA Ops:
  7.2 66.7 %copy-start.2 = (bf16[2048,256]{1,0:T(8,128)(2,1)S(1)}, bf16[2048,256]{1,0:T(8,128)(2,1)}, u32[]{:S(2)}) copy-start(bf16[2048,256]{1,0:T(8,128)(2,1)} %w_ref.1) | copy-start | bytes 3145732
  7.2 66.7 %all-gather.3.cloned.1.call-start = ((), (), s32[]{:S(2)}) async-start(), calls=%async_computation.5 | async-start | bytes 4718592 | tf_op jit(solution)/shard_map/all_gather | solution.py:251
  7.9 140.7 %reduce-scatter.2.cloned.1.call-start = ((), (), s32[]{:S(2)}) async-start(), calls=%async_computation.4 | async-start | bytes 4718592 | tf_op jit(solution)/shard_map/reduce_scatter | solution.py:257
  73.9 2.2 %copy-start = (bf16[8192,256]{1,0:T(8,128)(2,1)S(1)}, bf16[8192,256]{1,0:T(8,128)(2,1)}, u32[]{:S(2)}) copy-start(bf16[8192,256]{1,0:T(8,128)(2,1)} %all-gather.3.cloned.1.call-done) | copy-start | bytes 12582916
  76.1 1.0 copy-start.3
  77.1 0.7 copy-start.4
  89.6 2.0 %copy-start.1 = (bf16[1024,2048]{1,0:T(8,128)(2,1)}, bf16[1024,2048]{1,0:T(8,128)(2,1)S(1)}, u32[]{:S(2)}) copy-start(bf16[1024,2048]{1,0:T(8,128)(2,1)S(1)} %get-tuple-element.14) | copy-start | bytes 12582916
Sparse Core Ops, SparseCore 0:
  10.1 63.7 all-gather.2
  91.7 56.8 reduce-scatter.1

commit v2 on v1

--- a/solution.py
+++ b/solution.py
@@ -114,7 +114,7 @@
     )(wanted, back)
 
 
-def attend(owners, tokens, q_weight, cotangent, got):
+def attend(rows_at, owners, me, tokens, q_weight, cotangent, got, carried, ring):
     seq_len, width = cotangent.shape
     mp_count = tokens.shape[0]
     dp_count, nei, _ = got.shape
@@ -122,40 +122,56 @@
     picks = owners.shape[0]
     span_keys = NEIGH * nei
     tile_keys = 3 * span_keys
-    blocks = seq_len // BLOCK
+    low, high = rows_at
+    count = high - low
+    blocks = count // BLOCK
+    key_low = low // SPAN * span_keys
+    key_rows = count // SPAN * span_keys + span_keys
     scaling = 1.0 / math.sqrt(DH)
-
-    def kernel(
-        own_ref, tok_hbm, w_ref, cot_hbm, got_ref, att_ref, term_hbm, use_ref,
-        tok_ref, cot_ref, term_ref, q_ref, qg_ref, k_ref, v_ref, ku_ref, vu_ref, in_sem, cot_sem, out_sem,
-    ):
+    n_extra = len(carried)
+
+    def kernel(own_ref, me_ref, tok_hbm, w_ref, cot_hbm, got_ref, *refs):
+        carried_refs, refs = refs[:n_extra], refs[n_extra:]
+        att_hbm = refs[0]
+        if ring:
+            use_ref, target_refs = refs[1], refs[2 : 2 + len(ring)]
+            refs = refs[2 + len(ring) :]
+            ku_ref, vu_ref = refs[-2:]
+        else:
+            term_hbm, ku_ref, vu_ref = refs[1:4]
+            refs = refs[4:]
+        tok_ref, cot_ref, att_ref, term_ref, q_ref, qg_ref, k_ref, v_ref = refs[:8]
+        in_sem, cot_sem, att_sem, out_sem = refs[8:12]
+
         def load(b):
             rows = slice(b * BLOCK, (b + 1) * BLOCK)
-            return pltpu.make_async_copy(tok_hbm.at[:, rows, :], tok_ref.at[:, rows, :], in_sem.at[b])
+            source = tok_hbm.at[:, slice(low + b * BLOCK, low + (b + 1) * BLOCK), :]
+            return pltpu.make_async_copy(source, tok_ref.at[:, rows, :], in_sem.at[b])
 
         def store(b):
             rows = slice(b * BLOCK, (b + 1) * BLOCK)
             return pltpu.make_async_copy(term_ref.at[rows, :], term_hbm.at[rows, :], out_sem.at[b])
 
         load(0).start()
-        load_cot = pltpu.make_async_copy(cot_hbm, cot_ref, cot_sem)
+        load_cot = pltpu.make_async_copy(cot_hbm.at[low:high, :], cot_ref, cot_sem)
         load_cot.start()
         for b in range(1, blocks):
             load(b).start()
-        k_ref[:span_keys, :] = jnp.zeros((span_keys, width), BF16)
-        v_ref[:span_keys, :] = jnp.zeros((span_keys, width), BF16)
+        if low == 0:
+            k_ref[:span_keys, :] = jnp.zeros((span_keys, width), BF16)
+            v_ref[:span_keys, :] = jnp.zeros((span_keys, width), BF16)
         for n in range(picks):
-            at = span_keys + n * nei
-            k_ref[at : at + nei, :] = got_ref[own_ref[n], :, :width]
-            v_ref[at : at + nei, :] = got_ref[own_ref[n], :, width:]
-        use_ref[...] = jnp.zeros_like(use_ref)
+            at = span_keys + n * nei - key_low
+            if 0 <= at < key_rows:
+                k_ref[at : at + nei, :] = got_ref[own_ref[n], :, :width]
+                v_ref[at : at + nei, :] = got_ref[own_ref[n], :, width:]
         key_at = lax.broadcasted_iota(jnp.int32, (tile_keys, TILE), 0) // span_keys
         span_of = (lax.broadcasted_iota(jnp.int32, (tile_keys, TILE), 1) + 1) // SPAN
         inner = key_at == span_of
         first_tile = inner & (key_at > 0)
 
         def one_tile(t):
-            mask = inner if t else first_tile
+            mask = first_tile if low == 0 and t == 0 else inner
             rows = slice(t * TILE, (t + 1) * TILE)
             start = t * NEIGH * span_keys
             keys_at = slice(start, start + tile_keys)
@@ -203,60 +219,130 @@
             for t in range(b * BLOCK // TILE, (b + 1) * BLOCK // TILE):
                 one_tile(t)
             qg = qg_ref[rows, :]
-            for j in range(mp_count):
-                at = slice(j * width, (j + 1) * width)
-                term_ref[rows, at] = dot_nt(qg, w_ref[at, :]).astype(BF16)
-            store(b).start()
-        for n in range(picks):
-            at = span_keys + n * nei
-            use_ref[own_ref[n], :, :width] = (ku_ref[at : at + nei, :] * scaling).astype(BF16)
-            use_ref[own_ref[n], :, width:] = vu_ref[at : at + nei, :].astype(BF16)
-        for b in range(blocks):
-            store(b).wait()
-
-    padded = (seq_len // SPAN + 1) * span_keys
+            if not ring:
+                for j in range(mp_count):
+                    at = slice(j * width, (j + 1) * width)
+                    term_ref[rows, at] = dot_nt(qg, w_ref[at, :]).astype(BF16)
+                store(b).start()
+            else:
+                for (offset, first, size), ref in zip(ring, target_refs):
+                    if first <= b * BLOCK < first + size:
+                        target = lax.rem(me_ref[0] + offset, mp_count)
+                        w = w_ref[pl.ds(pl.multiple_of(target * width, width), width), :]
+                        at = slice(b * BLOCK - first, (b + 1) * BLOCK - first)
+                        ref[at, :] = dot_nt(qg, w).astype(BF16)
+        keep = pltpu.make_async_copy(att_ref, att_hbm.at[low:high, :], att_sem)
+        keep.start()
+        if ring:
+            use_ref[...] = jnp.zeros_like(use_ref)
+            earlier_ku, earlier_vu = carried_refs[1:]
+            for n in range(picks):
+                at = span_keys + n * nei
+                key_use = value_use = None
+                if at < low // SPAN * span_keys + span_keys:
+                    key_use = earlier_ku[at : at + nei, :]
+                    value_use = earlier_vu[at : at + nei, :]
+                if at >= key_low:
+                    mine = slice(at - key_low, at - key_low + nei)
+                    key_use = ku_ref[mine, :] if key_use is None else key_use + ku_ref[mine, :]
+                    value_use = vu_ref[mine, :] if value_use is None else value_use + vu_ref[mine, :]
+                use_ref[own_ref[n], :, :width] = (key_use * scaling).astype(BF16)
+                use_ref[own_ref[n], :, width:] = value_use.astype(BF16)
+        else:
+            for b in range(blocks):
+                store(b).wait()
+        keep.wait()
+
+    sums = jax.ShapeDtypeStruct((key_rows, width), F32)
+    whole = jax.ShapeDtypeStruct((seq_len, width), BF16)
+    if ring:
+        outs = [whole, jax.ShapeDtypeStruct((dp_count, nei, 2 * width), BF16)]
+        outs += [jax.ShapeDtypeStruct((size, width), BF16) for _, _, size in ring]
+        specs = [HBM] + [VMEM] * (len(ring) + 1)
+        last = [pltpu.VMEM((key_rows, width), F32), pltpu.VMEM((key_rows, width), F32)]
+        aliases = {6: 0}
+    else:
+        outs = [whole, jax.ShapeDtypeStruct((count, mp_count * width), BF16), sums, sums]
+        specs = [HBM, HBM, VMEM, VMEM]
+        last = []
+        aliases = {}
     return pl.pallas_call(
         kernel,
-        out_shape=(
-            jax.ShapeDtypeStruct((seq_len, width), BF16),
-            jax.ShapeDtypeStruct((seq_len, mp_count * width), BF16),
-            jax.ShapeDtypeStruct((dp_count, nei, 2 * width), BF16),
-        ),
-        in_specs=[SMEM, HBM, VMEM, HBM, VMEM],
-        out_specs=(VMEM, HBM, VMEM),
+        out_shape=tuple(outs),
+        in_specs=[SMEM, SMEM, HBM, VMEM, HBM, VMEM] + ([HBM, VMEM, VMEM] if carried else []),
+        out_specs=tuple(specs),
         scratch_shapes=[
-            pltpu.VMEM((mp_count, seq_len, width), BF16),
-            pltpu.VMEM((seq_len, width), BF16),
-            pltpu.VMEM((seq_len, mp_count * width), BF16),
-            pltpu.VMEM((seq_len, width), BF16),
-            pltpu.VMEM((seq_len, width), BF16),
-            pltpu.VMEM((padded, width), BF16),
-            pltpu.VMEM((padded, width), BF16),
-            pltpu.VMEM((padded, width), F32),
-            pltpu.VMEM((padded, width), F32),
+            pltpu.VMEM((mp_count, count, width), BF16),
+            pltpu.VMEM((count, width), BF16),
+            pltpu.VMEM((count, width), BF16),
+            pltpu.VMEM((count if not ring else BLOCK, mp_count * width), BF16),
+            pltpu.VMEM((count, width), BF16),
+            pltpu.VMEM((count, width), BF16),
+            pltpu.VMEM((key_rows, width), BF16),
+            pltpu.VMEM((key_rows, width), BF16),
             pltpu.SemaphoreType.DMA((blocks,)),
             pltpu.SemaphoreType.DMA(()),
+            pltpu.SemaphoreType.DMA(()),
             pltpu.SemaphoreType.DMA((blocks,)),
-        ],
-        compiler_params=pltpu.CompilerParams(vmem_limit_bytes=24 * 1024 * 1024),
-        name="attend",
-    )(owners, tokens, q_weight, cotangent, got)
+        ]
+        + last,
+        input_output_aliases=aliases,
+        compiler_params=pltpu.CompilerParams(vmem_limit_bytes=60 * 1024 * 1024),
+        name="attend_last" if ring else "attend_first",
+    )(owners, me, tokens, q_weight, cotangent, got, *carried)
+
+
+def ring_targets(size, rows):
+    half = rows // 2
+    far = size // 2
+    out = [(far, 0, half), (far, half, half)]
+    for hop in range(far - 1, 0, -1):
+        out += [(hop, 0, rows), (size - hop, 0, rows)]
+    return out + [(0, 0, rows)]
+
+
+def ring_sum(terms, size):
+    def send(x, by):
+        return lax.ppermute(x, "mp", [(i, (i + by) % size) for i in range(size)])
+
+    def add(*xs):
+        return sum(x.astype(F32) for x in xs)
+
+    half = terms[0].shape[0]
+    right, left = send(terms[0], 1), send(terms[1], -1)
+    for hop in range(1, size // 2):
+        own_right, own_left = terms[2 * hop], terms[2 * hop + 1]
+        if hop == 1:
+            right = jnp.concatenate([add(own_right[:half], right), own_right[half:].astype(F32)])
+            left = jnp.concatenate([own_left[:half].astype(F32), add(own_left[half:], left)])
+        else:
+            right, left = add(own_right, right), add(own_left, left)
+        right, left = send(right.astype(BF16), 1), send(left.astype(BF16), -1)
+    return add(terms[-1], right, left).astype(BF16)
 
 
 def body(
     tokens, q_weight, snippet_keys, snippet_values, out_cotangent, neighbour_ids, snippet_slot
 ):
-    dp_count = lax.axis_size("dp")
+    dp_count, mp_count = lax.axis_size("dp"), lax.axis_size("mp")
+    seq_len = tokens.shape[0]
     snip_count = snippet_keys.shape[0]
     gathered = lax.all_gather(tokens, "mp", axis=0, tiled=False)
     request, owners = request_rows(neighbour_ids.T, snippet_slot, snip_count, dp_count)
     wanted = lax.all_to_all(request, "dp", split_axis=0, concat_axis=0, tiled=True)
     picked = pick_rows(wanted, snippet_keys, snippet_values)
     got = lax.all_to_all(picked, "dp", split_axis=0, concat_axis=0, tiled=True)
-    attended, terms, uses = attend(owners, gathered, q_weight, out_cotangent, got)
-    input_grad = lax.psum_scatter(terms, "mp", scatter_dimension=1, tiled=True)
+    me = lax.axis_index("mp").astype(jnp.int32).reshape(1)
+    split = seq_len // 2
+    shared = (owners, me, gathered, q_weight, out_cotangent, got)
+    attended, terms, *sums = attend((0, split), *shared, (), None)
+    input_grad_first = lax.psum_scatter(terms, "mp", scatter_dimension=1, tiled=True)
+    ring = ring_targets(mp_count, seq_len - split)
+    attended, uses, *targets = attend((split, seq_len), *shared, (attended, *sums), ring)
+    input_grad_last = ring_sum(targets, mp_count)
     back = lax.all_to_all(uses, "dp", split_axis=0, concat_axis=0, tiled=True)
     key_grad, value_grad = sum_uses(wanted, back, snip_count)
+    input_grad = jnp.concatenate([input_grad_first, input_grad_last], axis=0)
     return (attended, input_grad, key_grad, value_grad)
 
 

time: 156 us -> 167 us (1.071)
  the two profiles are of different devices: /device:TPU:1 before, /device:TPU:8 now
where the time goes in v2:
time: 167 us
  waiting for transfers between devices  55.7 us (33%)
  starting transfers between devices  42.4 us (25%)
  Pallas kernels  28 us (17%)
  blocking collectives  19.2 us (11%)
  between operations  14.3 us (9%)
  other arithmetic  4.09 us (2%)
  local copies, waits for them, and re-layouts  2.87 us (2%)
    all_to_all x1, waiting for transfers between devices, body(): got = lax.all_to_all(picked, 'dp', split_axis=0, concat_axis=0, tiled=True)  27.9 us
    ppermute x8, starting transfers between devices, send(): return lax.ppermute(x, 'mp', [(i, (i + by) % size) for i in range(size)])  27.8 us
    ppermute x8, waiting for transfers between devices, send(): return lax.ppermute(x, 'mp', [(i, (i + by) % size) for i in range(size)])  19.7 us
    pallas_call x2, Pallas kernels, attend(): pl.pallas_call(kernel, out_shape=tuple(outs), in_specs=[SMEM, SMEM, HBM,...  19.7 us
    all_to_all x1, blocking collectives, body(): lax.all_to_all(request, 'dp', split_axis=0, concat_axis=0, tiled=True)  19.2 us
    all_to_all x1, starting transfers between devices, body(): back = lax.all_to_all(uses, 'dp', split_axis=0, concat_axis=0, tiled=True)  8.92 us
    all_gather x1, waiting for transfers between devices, body(): gathered = lax.all_gather(tokens, 'mp', axis=0, tiled=False)  7.34 us
    all_to_all x1, starting transfers between devices, body(): got = lax.all_to_all(picked, 'dp', split_axis=0, concat_axis=0, tiled=True)  5.54 us
  transfers between devices with their start and end apart: 12, of which 8 were waited for; matrix products, arithmetic and copies ran while one was open for 2% of the time, Pallas kernels for 11%

profile of v2, /device:TPU:8, one launch (start us, length us, event | category | flops | bytes accessed | tf_op | source)
XLA Modules:
  0.0 166.5 jit_solution(2982915841126002519)
XLA Ops:
  7.9 2.5 %request_rows.1 = (s32[64,1,128]{2,1,0:T(1,128)}, s32[32]{0:T(128)}) custom-call(s32[2,16]{1,0:T(2,128)} %bitcast.5, s32[2048]{0:T(1024)} %slot_ref.1), custom_call_target="tpu_custom_call" | custom-call | tf_op jit(solution)/shard_map/request_rows/pallas_call | solution.py:52
  10.4 19.2 %all_to_all.15.want_ref = s32[64,1,128]{2,1,0:T(1,128)} all-to-all(s32[64,1,128]{2,1,0:T(1,128)} %get-tuple-element.24), channel_id=1, replica_groups=mesh['dp'=64,'mp'=8] {'dp'}, dimensions={0} | all-to-all | bytes 65536 | tf_op jit(solution)/shard_map/all_to_all | solution.py:332
  29.6 2.4 %pick_rows.1 = bf16[64,16,512]{2,1,0:T(8,128)(2,1)} custom-call(s32[64,1,128]{2,1,0:T(1,128)} %all_to_all.15.want_ref, bf16[32,16,256]{2,1,0:T(8,128)(2,1)} %key_ref.1, bf16[32,16,256]{2,1,0:T(8,128)(2,1)} %value_ref.1), custom_call_target="tpu_custom_call" | custom-call | tf_op jit(solution)/shard_map/pick_rows/pallas_call | solution.py:77
  32.0 5.5 %all-to-all-start.1 = ((bf16[64,16,512]{2,1,0:T(8,128)(2,1)}), bf16[64,16,512]{2,1,0:T(8,128)(2,1)S(1)}, u32[]{:S(2)}, u32[]{:S(2)}) async-start(bf16[64,16,512]{2,1,0:T(8,128)(2,1)} %pick_rows.1), calls=%async_computation.1 | async-start | bytes 2097152 | tf_op jit(solution)/shard_map/all_to_all | solution.py:334
  37.6 27.9 %all-to-all-done.1.got_ref = bf16[64,16,512]{2,1,0:T(8,128)(2,1)S(1)} async-done(((bf16[64,16,512]{2,1,0:T(8,128)(2,1)}), bf16[64,16,512]{2,1,0:T(8,128)(2,1)S(1)}, u32[]{:S(2)}, u32[]{:S(2)}) %all-to-all-start.1) | async-done | bytes 1048608 | tf_op jit(solution)/shard_map/all_to_all | solution.py:334
  65.6 7.3 %all-gather.3.cloned.1.call-done = bf16[8192,256]{1,0:T(8,128)(2,1)} async-done(((bf16[1024,256]{1,0:T(8,128)(2,1)}), bf16[8192,256]{1,0:T(8,128)(2,1)}) %all-gather.3.cloned.1.call-update) | async-done | bytes 4194320 | tf_op jit(solution)/shard_map/all_gather | solution.py:330
  72.9 9.5 %attend_first.1 = (bf16[1024,256]{1,0:T(8,128)(2,1)}, bf16[512,2048]{1,0:T(8,128)(2,1)}, f32[288,256]{1,0:T(8,128)}, f32[288,256]{1,0:T(8,128)}) custom-call(s32[32]{0:T(128)} %get-tuple-element.23.own_ref, s32[1]{0:T(128)} %bitcast.1.me_ref, bf16[8,1024,256]{2,1,0:T(8,128)(2,1)} %bitcast.3, bf16[2048,256]{1,0:T(8,128)(2,1)} %w_ref.3, ...), custom_call_target="tpu_custom_call" | custom-call | tf_op jit(solution)/shard_map/attend_first/pallas_call | solution.py:269
  82.4 10.2 %attend_last.1 = (bf16[1024,256]{1,0:T(8,128)(2,1)}, bf16[64,16,512]{2,1,0:T(8,128)(2,1)}, bf16[256,256]{1,0:T(8,128)(2,1)}, bf16[256,256]{1,0:T(8,128)(2,1)}, b...) custom-call(s32[32]{0:T(128)} %get-tuple-element.23.own_ref, ...), custom_call_target="tpu_custom_call", output_to_operand_aliasing={{0}: (6, {})} | custom-call | tf_op jit(solution)/shard_map/attend_last/pallas_call | solution.py:269
  92.7 4.7 %collective-permute-start.4 = (bf16[256,256]{1,0:T(8,128)(2,1)}, bf16[256,256]{1,0:T(8,128)(2,1)S(1)}, u32[]{:S(2)}, u32[]{:S(2)}) collective-permute-start(bf16[256,256]{1,0:T(8,128)(2,1)} %get-tuple-element.38), channel_id=1, source_target_pairs={{0,7},{1,0},{2,1},{3,2},{4,3},{5,4},{6,5},{7,6},{8,15},{9,8},{10,9... | collective-permute-start | bytes 393224 | tf_op jit(solution)/shard_map/ppermute | solution.py:306
  97.4 8.9 %all-to-all-start.2 = ((bf16[64,16,512]{2,1,0:T(8,128)(2,1)}), bf16[64,16,512]{2,1,0:T(8,128)(2,1)S(1)}, u32[]{:S(2)}, u32[]{:S(2)}) async-start(bf16[64,16,512]{2,1,0:T(8,128)(2,1)} %get-tuple-element.39), calls=%async_computation.3 | async-start | bytes 2097152 | tf_op jit(solution)/shard_map/all_to_all | solution.py:343
  108.2 2.7 %collective-permute-start = (bf16[256,256]{1,0:T(8,128)(2,1)}, bf16[256,256]{1,0:T(8,128)(2,1)S(1)}, u32[]{:S(2)}, u32[]{:S(2)}) collective-permute-start(bf16[256,256]{1,0:T(8,128)(2,1)} %get-tuple-element.34), channel_id=1, source_target_pairs={{0,1},{1,2},{2,3},{3,4},{4,5},{5,6},{6,7},{7,0},{8,9},{9,10},{10,1... | collective-permute-start | bytes 393224 | tf_op jit(solution)/shard_map/ppermute | solution.py:306
  111.8 4.4 %collective-permute-start.5 = (bf16[512,256]{1,0:T(8,128)(2,1)S(1)}, bf16[512,256]{1,0:T(8,128)(2,1)S(1)}, u32[]{:S(2)}, u32[]{:S(2)}) collective-permute-start(bf16[512,256]{1,0:T(8,128)(2,1)S(1)} %pad_maximum_fusion.2), channel_id=1, source_target_pairs={{0,7},{1,0},{2,1},{3,2},{4,3},{5,4},{6,5},{7,6},{8,15},{9,8},{10,9... | collective-permute-start | bytes 786440 | tf_op jit(solution)/shard_map/ppermute | solution.py:306
  116.2 3.9 %collective-permute-done = bf16[256,256]{1,0:T(8,128)(2,1)S(1)} collective-permute-done((bf16[256,256]{1,0:T(8,128)(2,1)}, bf16[256,256]{1,0:T(8,128)(2,1)S(1)}, u32[]{:S(2)}, u32[]{:S(2)}) %collective-permute-start) | collective-permute-done | bytes 131104 | tf_op jit(solution)/shard_map/ppermute | solution.py:306
  121.1 1.9 %collective-permute-start.1 = (bf16[512,256]{1,0:T(8,128)(2,1)S(1)}, bf16[512,256]{1,0:T(8,128)(2,1)S(1)}, u32[]{:S(2)}, u32[]{:S(2)}) collective-permute-start(bf16[512,256]{1,0:T(8,128)(2,1)S(1)} %pad_maximum_fusion.1), channel_id=1, source_target_pairs={{0,1},{1,2},{2,3},{3,4},{4,5},{5,6},{6,7},{7,0},{8,9},{9,10},{10,1... | collective-permute-start | bytes 786440 | tf_op jit(solution)/shard_map/ppermute | solution.py:306
  123.0 4.6 %collective-permute-done.5 = bf16[512,256]{1,0:T(8,128)(2,1)S(1)} collective-permute-done((bf16[512,256]{1,0:T(8,128)(2,1)S(1)}, bf16[512,256]{1,0:T(8,128)(2,1)S(1)}, u32[]{:S(2)}, u32[]{:S(2)}) %collective-permute-start.5) | collective-permute-done | bytes 262176 | tf_op jit(solution)/shard_map/ppermute | solution.py:306
  127.7 4.7 %collective-permute-start.6 = (bf16[512,256]{1,0:T(8,128)(2,1)S(1)}, bf16[512,256]{1,0:T(8,128)(2,1)S(1)}, u32[]{:S(2)}, u32[]{:S(2)}) collective-permute-start(bf16[512,256]{1,0:T(8,128)(2,1)S(1)} %add_convert_fusion.2), channel_id=1, source_target_pairs={{0,7},{1,0},{2,1},{3,2},{4,3},{5,4},{6,5},{7,6},{8,15},{9,8},{10,9... | collective-permute-start | bytes 786440 | tf_op jit(solution)/shard_map/ppermute | solution.py:306
  132.7 1.9 %collective-permute-start.2 = (bf16[512,256]{1,0:T(8,128)(2,1)S(1)}, bf16[512,256]{1,0:T(8,128)(2,1)S(1)}, u32[]{:S(2)}, u32[]{:S(2)}) collective-permute-start(bf16[512,256]{1,0:T(8,128)(2,1)S(1)} %add_convert_fusion.4), channel_id=1, source_target_pairs={{0,1},{1,2},{2,3},{3,4},{4,5},{5,6},{6,7},{7,0},{8,9},{9,10},{10,1... | collective-permute-start | bytes 786440 | tf_op jit(solution)/shard_map/ppermute | solution.py:306
  134.7 3.1 %collective-permute-done.6 = bf16[512,256]{1,0:T(8,128)(2,1)S(1)} collective-permute-done((bf16[512,256]{1,0:T(8,128)(2,1)S(1)}, bf16[512,256]{1,0:T(8,128)(2,1)S(1)}, u32[]{:S(2)}, u32[]{:S(2)}) %collective-permute-start.6) | collective-permute-done | bytes 262176 | tf_op jit(solution)/shard_map/ppermute | solution.py:306
  137.9 5.6 %collective-permute-start.7 = (bf16[512,256]{1,0:T(8,128)(2,1)S(1)}, bf16[512,256]{1,0:T(8,128)(2,1)S(1)}, u32[]{:S(2)}, u32[]{:S(2)}) collective-permute-start(bf16[512,256]{1,0:T(8,128)(2,1)S(1)} %add_convert_fusion.1), channel_id=1, source_target_pairs={{0,7},{1,0},{2,1},{3,2},{4,3},{5,4},{6,5},{7,6},{8,15},{9,8},{10,9... | collective-permute-start | bytes 786440 | tf_op jit(solution)/shard_map/ppermute | solution.py:306
  143.6 1.9 %collective-permute-start.3 = (bf16[512,256]{1,0:T(8,128)(2,1)S(1)}, bf16[512,256]{1,0:T(8,128)(2,1)S(1)}, u32[]{:S(2)}, u32[]{:S(2)}) collective-permute-start(bf16[512,256]{1,0:T(8,128)(2,1)S(1)} %add_convert_fusion.3), channel_id=1, source_target_pairs={{0,1},{1,2},{2,3},{3,4},{4,5},{5,6},{6,7},{7,0},{8,9},{9,10},{10,1... | collective-permute-start | bytes 786440 | tf_op jit(solution)/shard_map/ppermute | solution.py:306
  145.5 2.4 %collective-permute-done.7 = bf16[512,256]{1,0:T(8,128)(2,1)S(1)} collective-permute-done((bf16[512,256]{1,0:T(8,128)(2,1)S(1)}, bf16[512,256]{1,0:T(8,128)(2,1)S(1)}, u32[]{:S(2)}, u32[]{:S(2)}) %collective-permute-start.7) | collective-permute-done | bytes 262176 | tf_op jit(solution)/shard_map/ppermute | solution.py:306
  147.9 5.4 %collective-permute-done.3 = bf16[512,256]{1,0:T(8,128)(2,1)S(1)} collective-permute-done((bf16[512,256]{1,0:T(8,128)(2,1)S(1)}, bf16[512,256]{1,0:T(8,128)(2,1)S(1)}, u32[]{:S(2)}, u32[]{:S(2)}) %collective-permute-start.3) | collective-permute-done | bytes 262176 | tf_op jit(solution)/shard_map/ppermute | solution.py:306
  154.5 3.4 %sum_uses.1 = (f32[32,16,256]{2,1,0:T(8,128)}, f32[32,16,256]{2,1,0:T(8,128)}) custom-call(s32[64,1,128]{2,1,0:T(1,128)} %all_to_all.15.want_ref, bf16[64,16,512]{2,1,0:T(8,128)(2,1)} %copy-done.1), custom_call_target="tpu_custom_call" | custom-call | tf_op jit(solution)/shard_map/sum_uses/pallas_call | solution.py:108
  157.9 1.8 %pad_maximum_fusion = bf16[1024,256]{1,0:T(8,128)(2,1)} fusion(bf16[512,256]{1,0:T(8,128)(2,1)S(1)} %add_convert_fusion, bf16[512,256]{1,0:T(8,128)(2,1)} %reduce-scatter.2.cloned.1.call-done), kind=kLoop, calls=%fused_computation | loop fusion | flops 1048576 | bytes 1048576 | tf_op jit(solution)/shard_map/concatenate | solution.py:345
  (34 shorter events, 6.2 us)
Async XLA Ops:
  7.2 65.8 %all-gather.3.cloned.1.call-start = ((), (), s32[]{:S(2)}) async-start(), calls=%async_computation.5 | async-start | bytes 4718592 | tf_op jit(solution)/shard_map/all_gather | solution.py:330
  32.0 33.5 %all-to-all-start.1 = ((bf16[64,16,512]{2,1,0:T(8,128)(2,1)}), bf16[64,16,512]{2,1,0:T(8,128)(2,1)S(1)}, u32[]{:S(2)}, u32[]{:S(2)}) async-start(bf16[64,16,512]{2,1,0:T(8,128)(2,1)} %pick_rows.1), calls=%async_computation.1 | async-start | bytes 2097152 | tf_op jit(solution)/shard_map/all_to_all | solution.py:334
  37.6 120.3 %reduce-scatter.2.cloned.1.call-start = ((), (), s32[]{:S(2)}) async-start(), calls=%async_computation.4 | async-start | bytes 2359296 | tf_op jit(solution)/shard_map/reduce_scatter | solution.py:339
  65.6 7.3 %copy-start = (bf16[64,16,512]{2,1,0:T(8,128)(2,1)}, bf16[64,16,512]{2,1,0:T(8,128)(2,1)S(1)}, u32[]{:S(2)}) copy-start(bf16[64,16,512]{2,1,0:T(8,128)(2,1)S(1)} %all-to-all-done.1.got_ref) | copy-start | bytes 3145732
  92.7 34.9 %copy-start.5 = (bf16[512,256]{1,0:T(8,128)(2,1)S(1)}, bf16[512,256]{1,0:T(8,128)(2,1)}, u32[]{:S(2)}) copy-start(bf16[512,256]{1,0:T(8,128)(2,1)} %get-tuple-element.36) | copy-start | bytes 786436
  92.7 40.0 %copy-start.4 = (bf16[512,256]{1,0:T(8,128)(2,1)S(1)}, bf16[512,256]{1,0:T(8,128)(2,1)}, u32[]{:S(2)}) copy-start(bf16[512,256]{1,0:T(8,128)(2,1)} %get-tuple-element.32) | copy-start | bytes 786436
  92.7 45.1 %copy-start.3 = (bf16[512,256]{1,0:T(8,128)(2,1)S(1)}, bf16[512,256]{1,0:T(8,128)(2,1)}, u32[]{:S(2)}) copy-start(bf16[512,256]{1,0:T(8,128)(2,1)} %get-tuple-element.35) | copy-start | bytes 786436
  92.7 50.8 %copy-start.2 = (bf16[512,256]{1,0:T(8,128)(2,1)S(1)}, bf16[512,256]{1,0:T(8,128)(2,1)}, u32[]{:S(2)}) copy-start(bf16[512,256]{1,0:T(8,128)(2,1)} %get-tuple-element.31) | copy-start | bytes 786436
  92.7 60.7 %copy-start.6 = (bf16[512,256]{1,0:T(8,128)(2,1)S(1)}, bf16[512,256]{1,0:T(8,128)(2,1)}, u32[]{:S(2)}) copy-start(bf16[512,256]{1,0:T(8,128)(2,1)} %get-tuple-element.30) | copy-start | bytes 786436
  92.7 18.1 %collective-permute-start.4 = (bf16[256,256]{1,0:T(8,128)(2,1)}, bf16[256,256]{1,0:T(8,128)(2,1)S(1)}, u32[]{:S(2)}, u32[]{:S(2)}) collective-permute-start(bf16[256,256]{1,0:T(8,128)(2,1)} %get-tuple-element.38), channel_id=1, source_target_pairs={{0,7},{1,0},{2,1},{3,2},{4,3},{5,4},{6,5},{7,6},{8,15},{9,8},{10,9... | collective-permute-start | bytes 393224 | tf_op jit(solution)/shard_map/ppermute | solution.py:306
  97.4 56.1 %all-to-all-start.2 = ((bf16[64,16,512]{2,1,0:T(8,128)(2,1)}), bf16[64,16,512]{2,1,0:T(8,128)(2,1)S(1)}, u32[]{:S(2)}, u32[]{:S(2)}) async-start(bf16[64,16,512]{2,1,0:T(8,128)(2,1)} %get-tuple-element.39), calls=%async_computation.3 | async-start | bytes 2097152 | tf_op jit(solution)/shard_map/all_to_all | solution.py:343
  108.2 11.9 %collective-permute-start = (bf16[256,256]{1,0:T(8,128)(2,1)}, bf16[256,256]{1,0:T(8,128)(2,1)S(1)}, u32[]{:S(2)}, u32[]{:S(2)}) collective-permute-start(bf16[256,256]{1,0:T(8,128)(2,1)} %get-tuple-element.34), channel_id=1, source_target_pairs={{0,1},{1,2},{2,3},{3,4},{4,5},{5,6},{6,7},{7,0},{8,9},{9,10},{10,1... | collective-permute-start | bytes 393224 | tf_op jit(solution)/shard_map/ppermute | solution.py:306
  111.8 15.8 %collective-permute-start.5 = (bf16[512,256]{1,0:T(8,128)(2,1)S(1)}, bf16[512,256]{1,0:T(8,128)(2,1)S(1)}, u32[]{:S(2)}, u32[]{:S(2)}) collective-permute-start(bf16[512,256]{1,0:T(8,128)(2,1)S(1)} %pad_maximum_fusion.2), channel_id=1, source_target_pairs={{0,7},{1,0},{2,1},{3,2},{4,3},{5,4},{6,5},{7,6},{8,15},{9,8},{10,9... | collective-permute-start | bytes 786440 | tf_op jit(solution)/shard_map/ppermute | solution.py:306
  121.1 11.6 %collective-permute-start.1 = (bf16[512,256]{1,0:T(8,128)(2,1)S(1)}, bf16[512,256]{1,0:T(8,128)(2,1)S(1)}, u32[]{:S(2)}, u32[]{:S(2)}) collective-permute-start(bf16[512,256]{1,0:T(8,128)(2,1)S(1)} %pad_maximum_fusion.1), channel_id=1, source_target_pairs={{0,1},{1,2},{2,3},{3,4},{4,5},{5,6},{6,7},{7,0},{8,9},{9,10},{10,1... | collective-permute-start | bytes 786440 | tf_op jit(solution)/shard_map/ppermute | solution.py:306
  127.7 10.1 %collective-permute-start.6 = (bf16[512,256]{1,0:T(8,128)(2,1)S(1)}, bf16[512,256]{1,0:T(8,128)(2,1)S(1)}, u32[]{:S(2)}, u32[]{:S(2)}) collective-permute-start(bf16[512,256]{1,0:T(8,128)(2,1)S(1)} %add_convert_fusion.2), channel_id=1, source_target_pairs={{0,7},{1,0},{2,1},{3,2},{4,3},{5,4},{6,5},{7,6},{8,15},{9,8},{10,9... | collective-permute-start | bytes 786440 | tf_op jit(solution)/shard_map/ppermute | solution.py:306
  132.7 10.8 %collective-permute-start.2 = (bf16[512,256]{1,0:T(8,128)(2,1)S(1)}, bf16[512,256]{1,0:T(8,128)(2,1)S(1)}, u32[]{:S(2)}, u32[]{:S(2)}) collective-permute-start(bf16[512,256]{1,0:T(8,128)(2,1)S(1)} %add_convert_fusion.4), channel_id=1, source_target_pairs={{0,1},{1,2},{2,3},{3,4},{4,5},{5,6},{6,7},{7,0},{8,9},{9,10},{10,1... | collective-permute-start | bytes 786440 | tf_op jit(solution)/shard_map/ppermute | solution.py:306
  137.9 10.1 %collective-permute-start.7 = (bf16[512,256]{1,0:T(8,128)(2,1)S(1)}, bf16[512,256]{1,0:T(8,128)(2,1)S(1)}, u32[]{:S(2)}, u32[]{:S(2)}) collective-permute-start(bf16[512,256]{1,0:T(8,128)(2,1)S(1)} %add_convert_fusion.1), channel_id=1, source_target_pairs={{0,7},{1,0},{2,1},{3,2},{4,3},{5,4},{6,5},{7,6},{8,15},{9,8},{10,9... | collective-permute-start | bytes 786440 | tf_op jit(solution)/shard_map/ppermute | solution.py:306
  143.6 9.8 %collective-permute-start.3 = (bf16[512,256]{1,0:T(8,128)(2,1)S(1)}, bf16[512,256]{1,0:T(8,128)(2,1)S(1)}, u32[]{:S(2)}, u32[]{:S(2)}) collective-permute-start(bf16[512,256]{1,0:T(8,128)(2,1)S(1)} %add_convert_fusion.3), channel_id=1, source_target_pairs={{0,1},{1,2},{2,3},{3,4},{4,5},{5,6},{6,7},{7,0},{8,9},{9,10},{10,1... | collective-permute-start | bytes 786440 | tf_op jit(solution)/shard_map/ppermute | solution.py:306
  153.5 1.0 copy-start.1
Sparse Core Ops, SparseCore 0:
  10.1 62.8 all-gather.2
  82.6 47.8 reduce-scatter.1

commit v3 on v1

v3 whole, which is shorter than its diff:
```python
import math

import jax
import jax.numpy as jnp
from jax import lax
from jax.experimental import pallas as pl
from jax.experimental.pallas import tpu as pltpu
from jax.sharding import PartitionSpec as P

DH = 128
SPAN = 64
NEIGH = 2
TILE = 2 * SPAN
BLOCK = 2 * TILE
LANES = 128
F32 = jnp.float32
BF16 = jnp.bfloat16

VMEM = pl.BlockSpec(memory_space=pltpu.MemorySpace.VMEM)
SMEM = pl.BlockSpec(memory_space=pltpu.MemorySpace.SMEM)
HBM = pl.BlockSpec(memory_space=pltpu.MemorySpace.HBM)


def dot_nt(a, b):
    return lax.dot_general(a, b, (((1,), (1,)), ((), ())), preferred_element_type=F32)


def dot_tn(a, b):
    return lax.dot_general(a, b, (((0,), (0,)), ((), ())), preferred_element_type=F32)


def request_rows(ids, slot_table, snip_count, dp_count):
    spans = ids.shape[1]

    def kernel(ids_ref, slot_ref, req_ref, own_ref):
        def clear(i, c):
            req_ref[i, 0, 0] = 0
            return c

        lax.fori_loop(0, dp_count, clear, 0)

        def step(i, c):
            for n in range(NEIGH):
                slot = slot_ref[ids_ref[n, i]]
                owner = lax.div(slot, snip_count)
                req_ref[owner, 0, 0] = slot - owner * snip_count + 1
                own_ref[i * NEIGH + n] = owner
            return c

        lax.fori_loop(0, spans, step, 0)

    return pl.pallas_call(
        kernel,
        out_shape=(
            jax.ShapeDtypeStruct((dp_count, 1, LANES), jnp.int32),
            jax.ShapeDtypeStruct((spans * NEIGH,), jnp.int32),
        ),
        in_specs=[SMEM, SMEM],
        out_specs=(SMEM, SMEM),
        name="request_rows",
    )(ids, slot_table)


def pick_rows(wanted, keys, values):
    dp_count = wanted.shape[0]
    _, nei, width = keys.shape

    def kernel(want_ref, key_ref, value_ref, out_ref):
        def step(i, c):
            row = jnp.maximum(want_ref[i, 0, 0] - 1, 0)
            out_ref[i, :, :width] = key_ref[row]
            out_ref[i, :, width:] = value_ref[row]
            return c

        lax.fori_loop(0, dp_count, step, 0, unroll=4)

    return pl.pallas_call(
        kernel,
        out_shape=jax.ShapeDtypeStruct((dp_count, nei, 2 * width), keys.dtype),
        in_specs=[SMEM, VMEM, VMEM],
        out_specs=VMEM,
        name="pick_rows",
    )(wanted, keys, values)


def sum_uses(wanted, back, snip_count):
    dp_count, nei, twice = back.shape
    width = twice // 2

    def kernel(want_ref, back_ref, key_ref, value_ref):
        key_ref[...] = jnp.zeros_like(key_ref)
        value_ref[...] = jnp.zeros_like(value_ref)

        def step(i, c):
            want = want_ref[i, 0, 0]

            @pl.when(want > 0)
            def _():
                row = jnp.maximum(want - 1, 0)
                key_ref[row] += back_ref[i, :, :width].astype(F32)
                value_ref[row] += back_ref[i, :, width:].astype(F32)

            return c

        lax.fori_loop(0, dp_count, step, 0)

    out = jax.ShapeDtypeStruct((snip_count, nei, width), F32)
    return pl.pallas_call(
        kernel,
        out_shape=(out, out),
        in_specs=[SMEM, VMEM],
        out_specs=(VMEM, VMEM),
        name="sum_uses",
    )(wanted, back)


def tile_keys_of(t, span_keys):
    start = t * (TILE // SPAN) * span_keys
    return slice(start, start + (TILE // SPAN + 1) * span_keys)


def prepare(owners, cotangent, got):
    seq_len, width = cotangent.shape
    nei = got.shape[1]
    heads = width // DH
    picks = owners.shape[0]
    span_keys = NEIGH * nei
    tiles = seq_len // TILE
    padded = (seq_len // SPAN + 1) * span_keys
    tile_keys = (TILE // SPAN + 1) * span_keys

    def kernel(own_ref, cot_ref, got_ref, v_ref, k_ref, pg_ref):
        k_ref[:span_keys, :] = jnp.zeros((span_keys, width), BF16)
        v_ref[:span_keys, :] = jnp.zeros((span_keys, width), BF16)
        for n in range(picks):
            at = span_keys + n * nei
            k_ref[at : at + nei, :] = got_ref[own_ref[n], :, :width]
            v_ref[at : at + nei, :] = got_ref[own_ref[n], :, width:]
        for t in range(tiles):
            rows = slice(t * TILE, (t + 1) * TILE)
            for h in range(heads):
                cols = slice(h * DH, (h + 1) * DH)
                pg_ref[t * heads + h] = dot_nt(v_ref[tile_keys_of(t, span_keys), cols], cot_ref[rows, cols])

    return pl.pallas_call(
        kernel,
        out_shape=(
            jax.ShapeDtypeStruct((padded, width), BF16),
            jax.ShapeDtypeStruct((padded, width), BF16),
            jax.ShapeDtypeStruct((tiles * heads, tile_keys, TILE), F32),
        ),
        in_specs=[SMEM, VMEM, VMEM],
        out_specs=(VMEM, VMEM, VMEM),
        compiler_params=pltpu.CompilerParams(vmem_limit_bytes=16 * 1024 * 1024),
        name="prepare",
    )(owners, cotangent, got)


def attend(tokens, q_weight, keys, prob_grads, seq_len, span_keys):
    mp_count, _, width = tokens.shape
    heads = width // DH
    blocks = seq_len // BLOCK
    tile_keys = prob_grads.shape[1]
    scaling = 1.0 / math.sqrt(DH)

    def kernel(
        tok_hbm, w_ref, k_ref, pg_ref, term_hbm, q_hbm, pair_hbm,
        tok_ref, term_ref, q_ref, pair_ref, qg_ref, in_sem, out_sem, keep_sem,
    ):
        def load(b):
            rows = slice(b * BLOCK, (b + 1) * BLOCK)
            return pltpu.make_async_copy(tok_hbm.at[:, rows, :], tok_ref.at[:, rows, :], in_sem.at[b])

        def store(b):
            rows = slice(b * BLOCK, (b + 1) * BLOCK)
            return pltpu.make_async_copy(term_ref.at[rows, :], term_hbm.at[rows, :], out_sem.at[b])

        for b in range(blocks):
            load(b).start()
        key_at = lax.broadcasted_iota(jnp.int32, (tile_keys, TILE), 0) // span_keys
        span_of = (lax.broadcasted_iota(jnp.int32, (tile_keys, TILE), 1) + 1) // SPAN
        inner = key_at == span_of
        first_tile = inner & (key_at > 0)

        def one_tile(t):
            rows = slice(t * TILE, (t + 1) * TILE)
            for h in range(heads):
                cols = slice(h * DH, (h + 1) * DH)
                k = k_ref[tile_keys_of(t, span_keys), cols]
                scores = dot_nt(k, q_ref[rows, cols]) * scaling
                scores = jnp.where(inner if t else first_tile, scores, -jnp.inf)
                top = jnp.max(scores, axis=0, keepdims=True)
                if t == 0:
                    top = jnp.where(top == -jnp.inf, 0.0, top)
                grown = jnp.exp(scores - top)
                total = jnp.sum(grown, axis=0, keepdims=True)
                if t == 0:
                    total = jnp.where(total > 0.0, total, 1.0)
                weights = grown * (1.0 / total)
                prob_grad = pg_ref[t * heads + h]
                row_delta = jnp.sum(weights * prob_grad, axis=0, keepdims=True)
                score_grad = (weights * (prob_grad - row_delta)).astype(BF16)
                pair_ref[0, t * heads + h] = weights.astype(BF16)
                pair_ref[1, t * heads + h] = score_grad
                qg_ref[rows, cols] = (dot_tn(score_grad, k) * scaling).astype(BF16)

        for b in range(blocks):
            rows = slice(b * BLOCK, (b + 1) * BLOCK)
            load(b).wait()
            x = jnp.concatenate([tok_ref[j, rows, :] for j in range(mp_count)], axis=1)
            q_ref[rows, :] = jnp.dot(x, w_ref[...], preferred_element_type=F32).astype(BF16)
            for t in range(b * BLOCK // TILE, (b + 1) * BLOCK // TILE):
                one_tile(t)
            if b == blocks - 1:
                keep = [
                    pltpu.make_async_copy(q_ref, q_hbm, keep_sem.at[0]),
                    pltpu.make_async_copy(pair_ref, pair_hbm, keep_sem.at[1]),
                ]
                for copy in keep:
                    copy.start()
            term_ref[rows, :] = dot_nt(qg_ref[rows, :], w_ref[...]).astype(BF16)
            store(b).start()
        for b in range(blocks):
            store(b).wait()
        for copy in keep:
            copy.wait()

    return pl.pallas_call(
        kernel,
        out_shape=(
            pltpu.HBM((seq_len, mp_count * width), BF16),
            pltpu.HBM((seq_len, width), BF16),
            pltpu.HBM((2, *prob_grads.shape), BF16),
        ),
        in_specs=[HBM, VMEM, VMEM, VMEM],
        out_specs=(HBM, HBM, HBM),
        scratch_shapes=[
            pltpu.VMEM((mp_count, seq_len, width), BF16),
            pltpu.VMEM((seq_len, mp_count * width), BF16),
            pltpu.VMEM((seq_len, width), BF16),
            pltpu.VMEM((2, *prob_grads.shape), BF16),
            pltpu.VMEM((seq_len, width), BF16),
            pltpu.SemaphoreType.DMA((blocks,)),
            pltpu.SemaphoreType.DMA((blocks,)),
            pltpu.SemaphoreType.DMA((2,)),
        ],
        compiler_params=pltpu.CompilerParams(vmem_limit_bytes=24 * 1024 * 1024),
        name="attend",
    )(pltpu.with_memory_space_constraint(tokens, pltpu.HBM), q_weight, keys, prob_grads)


def finish(owners, queries, pairs, values, cotangent, dp_count):
    seq_len, width = cotangent.shape
    heads = width // DH
    tiles = seq_len // TILE
    picks = owners.shape[0]
    span_keys = values.shape[0] // (seq_len // SPAN + 1)
    nei = span_keys // NEIGH
    scaling = 1.0 / math.sqrt(DH)

    def kernel(own_ref, q_ref, pair_ref, v_ref, cot_ref, att_ref, use_ref, ku_ref, vu_ref):
        use_ref[...] = jnp.zeros_like(use_ref)
        for t in range(tiles):
            rows = slice(t * TILE, (t + 1) * TILE)
            keys_at = tile_keys_of(t, span_keys)
            start, mid, end = keys_at.start, keys_at.start + span_keys, keys_at.stop
            for h in range(heads):
                cols = slice(h * DH, (h + 1) * DH)
                p = pair_ref[0, t * heads + h]
                key_use = jnp.dot(pair_ref[1, t * heads + h], q_ref[rows, cols], preferred_element_type=F32)
                value_use = jnp.dot(p, cot_ref[rows, cols], preferred_element_type=F32)
                att_ref[rows, cols] = dot_tn(p, v_ref[keys_at, cols]).astype(BF16)
                if t == 0:
                    ku_ref[start:mid, cols] = key_use[:span_keys]
                    vu_ref[start:mid, cols] = value_use[:span_keys]
                else:
                    ku_ref[start:mid, cols] += key_use[:span_keys]
                    vu_ref[start:mid, cols] += value_use[:span_keys]
                ku_ref[mid:end, cols] = key_use[span_keys:]
                vu_ref[mid:end, cols] = value_use[span_keys:]
        for n in range(picks):
            at = span_keys + n * nei
            use_ref[own_ref[n], :, :width] = (ku_ref[at : at + nei, :] * scaling).astype(BF16)
            use_ref[own_ref[n], :, width:] = vu_ref[at : at + nei, :].astype(BF16)

    return pl.pallas_call(
        kernel,
        out_shape=(
            jax.ShapeDtypeStruct((seq_len, width), BF16),
            jax.ShapeDtypeStruct((dp_count, nei, 2 * width), BF16),
        ),
        in_specs=[SMEM] + [VMEM] * 4,
        out_specs=(VMEM, VMEM),
        scratch_shapes=[pltpu.VMEM(values.shape, F32), pltpu.VMEM(values.shape, F32)],
        compiler_params=pltpu.CompilerParams(vmem_limit_bytes=16 * 1024 * 1024),
        name="finish",
    )(owners, queries, pairs, values, cotangent)


def body(
    tokens, q_weight, snippet_keys, snippet_values, out_cotangent, neighbour_ids, snippet_slot
):
    dp_count = lax.axis_size("dp")
    seq_len = tokens.shape[0]
    snip_count, nei, _ = snippet_keys.shape
    gathered = lax.all_gather(tokens, "mp", axis=0, tiled=False)
    request, owners = request_rows(neighbour_ids.T, snippet_slot, snip_count, dp_count)
    wanted = lax.all_to_all(request, "dp", split_axis=0, concat_axis=0, tiled=True)
    picked = pick_rows(wanted, snippet_keys, snippet_values)
    got = lax.all_to_all(picked, "dp", split_axis=0, concat_axis=0, tiled=True)
    values, keys, prob_grads = prepare(owners, out_cotangent, got)
    terms, queries, pairs = attend(
        gathered, q_weight, keys, prob_grads, seq_len, NEIGH * nei
    )
    input_grad = lax.psum_scatter(terms, "mp", scatter_dimension=1, tiled=True)
    attended, uses = finish(
        owners, queries, pairs, values, out_cotangent, dp_count
    )
    back = lax.all_to_all(uses, "dp", split_axis=0, concat_axis=0, tiled=True)
    key_grad, value_grad = sum_uses(wanted, back, snip_count)
    return (attended, input_grad, key_grad, value_grad)


def solution(mesh):
    return jax.shard_map(
        body,
        mesh=mesh,
        in_specs=(
            P("dp", "mp"),
            P(None, "mp"),
            P("dp", None, "mp"),
            P("dp", None, "mp"),
            P("dp", "mp"),
            P("dp", None),
            P(),
        ),
        out_specs=(P("dp", "mp"), P("dp", "mp"), P("dp", None, "mp"), P("dp", None, "mp")),
        check_vma=False,
    )
```

time: 156 us -> 150 us (0.962)
  waiting for transfers between devices: 23.1 us -> 18.3 us
  local copies, waits for them, and re-layouts: 5.84 us -> 1.9 us
  Pallas kernels: 20.2 us -> 23.4 us
    unnamed x10 -> x12, local copies, waits for them, and re-layouts: 5.84 us -> 1.9 us
    pallas_call x1 -> x3, Pallas kernels: 11.9 us -> 15.1 us  [the longest x1 12.2 us: attend(): pl.pallas_call(kernel, out_shape=(pltpu.HBM((seq_len, mp_count * width),...]
    reduce_scatter x1, waiting for transfers between devices: 15.3 us -> 12.2 us  [body(): input_grad = lax.psum_scatter(terms, 'mp', scatter_dimension=1, tiled=True)]
    all_gather x1, waiting for transfers between devices: 7.05 us -> 5.37 us  [body(): gathered = lax.all_gather(tokens, 'mp', axis=0, tiled=False)]
  transfers between devices with their start and end apart: 2 -> 2, of which waited for: 2 -> 2; matrix products, arithmetic and copies ran while one was open for 0% -> 0% of each run, Pallas kernels for 5% -> 7%
where the time goes in v3:
time: 150 us
  blocking collectives  92.2 us (61%)
  Pallas kernels  23.4 us (16%)
  waiting for transfers between devices  18.3 us (12%)
  between operations  14.1 us (9%)
  local copies, waits for them, and re-layouts  1.9 us (1%)
    all_to_all x1, blocking collectives, body(): back = lax.all_to_all(uses, 'dp', split_axis=0, concat_axis=0, tiled=True)  38.3 us
    all_to_all x1, blocking collectives, body(): got = lax.all_to_all(picked, 'dp', split_axis=0, concat_axis=0, tiled=True)  32.8 us
    all_to_all x1, blocking collectives, body(): lax.all_to_all(request, 'dp', split_axis=0, concat_axis=0, tiled=True)  21.2 us
    reduce_scatter x1, waiting for transfers between devices, body(): input_grad = lax.psum_scatter(terms, 'mp', scatter_dimension=1, tiled=True)  12.2 us
    pallas_call x1, Pallas kernels, attend(): pl.pallas_call(kernel, out_shape=(pltpu.HBM((seq_len, mp_count * width),...  12.2 us
    all_gather x1, waiting for transfers between devices, body(): gathered = lax.all_gather(tokens, 'mp', axis=0, tiled=False)  5.37 us
    pallas_call x1, Pallas kernels, sum_uses(): pl.pallas_call(kernel, out_shape=(out, out), in_specs=[SMEM, VMEM], out_s...  3.41 us
  transfers between devices with their start and end apart: 2, of which 2 were waited for; matrix products, arithmetic and copies ran while one was open for 0% of the time, Pallas kernels for 7%

profile of v3, /device:TPU:1, one launch (start us, length us, event | category | flops | bytes accessed | tf_op | source)
XLA Modules:
  0.0 150.0 jit_solution(10028602623784304142)
XLA Ops:
  7.2 0.0 copy-start
  7.2 0.0 copy-start.1
  7.2 0.0 all-gather.3.cloned.1.call-start
  7.2 0.7 all-gather.3.cloned.1.call-update
  7.9 0.0 reduce-scatter.2.cloned.1.call-start
  8.0 2.5 %request_rows.1 = (s32[64,1,128]{2,1,0:T(1,128)}, s32[32]{0:T(128)}) custom-call(s32[2,16]{1,0:T(2,128)} %bitcast.3, s32[2048]{0:T(1024)} %slot_ref.1), custom_call_target="tpu_custom_call" | custom-call | tf_op jit(solution)/shard_map/request_rows/pallas_call | solution.py:52
  10.5 21.2 %all_to_all.15.want_ref = s32[64,1,128]{2,1,0:T(1,128)} all-to-all(s32[64,1,128]{2,1,0:T(1,128)} %get-tuple-element.17), channel_id=1, replica_groups=mesh['dp'=64,'mp'=8] {'dp'}, dimensions={0} | all-to-all | bytes 65536 | tf_op jit(solution)/shard_map/all_to_all | solution.py:308
  31.7 2.4 %pick_rows.1 = bf16[64,16,512]{2,1,0:T(8,128)(2,1)} custom-call(s32[64,1,128]{2,1,0:T(1,128)} %all_to_all.15.want_ref, bf16[32,16,256]{2,1,0:T(8,128)(2,1)} %key_ref.1, bf16[32,16,256]{2,1,0:T(8,128)(2,1)} %value_ref.1), custom_call_target="tpu_custom_call" | custom-call | tf_op jit(solution)/shard_map/pick_rows/pallas_call | solution.py:77
  34.0 32.8 %all_to_all.16.got_ref = bf16[64,16,512]{2,1,0:T(8,128)(2,1)S(1)} all-to-all(bf16[64,16,512]{2,1,0:T(8,128)(2,1)} %pick_rows.1), channel_id=1, replica_groups=mesh['dp'=64,'mp'=8] {'dp'}, dimensions={0} | all-to-all | bytes 2097152 | tf_op jit(solution)/shard_map/all_to_all | solution.py:310
  66.8 0.0 copy-done
  66.8 0.7 copy-done.4
  67.5 1.0 prepare.1
  68.5 5.4 %all-gather.3.cloned.1.call-done = bf16[8192,256]{1,0:T(8,128)(2,1)} async-done(((bf16[1024,256]{1,0:T(8,128)(2,1)}), bf16[8192,256]{1,0:T(8,128)(2,1)}) %all-gather.3.cloned.1.call-update) | async-done | bytes 4194320 | tf_op jit(solution)/shard_map/all_gather | solution.py:306
  73.9 0.0 copy-done.1
  73.9 12.2 %attend.1 = (bf16[1024,2048]{1,0:T(8,128)(2,1)}, bf16[1024,256]{1,0:T(8,128)(2,1)}, bf16[2,16,96,128]{3,2,1,0:T(8,128)(2,1)}) custom-call(bf16[8,1024,256]{2,1,0:T(8,128)(2,1)} %bitcast.2, bf16[2048,256]{1,0:T(8,128)(2,1)S(1)} %copy-done.1, bf16[544,256]{1,0:T(8,128)(2,1)S(1)} %get-tuple-element.18.k_ref, f32[16,96,128]{2,1,0:T(8,128)S(1)} %get-tuple-element.19.pg_ref), custom_call_target="tpu_custom_call" | custom-call | tf_op jit(solution)/shard_map/attend/pallas_call | solution.py:228
  86.1 0.0 copy-start.3
  86.1 0.0 reduce-scatter.2.cloned.1.call-update
  86.1 0.0 copy-done.5
  86.1 1.1 copy-done.2
  87.2 0.1 copy-done.3
  87.4 1.9 %finish.1 = (bf16[1024,256]{1,0:T(8,128)(2,1)}, bf16[64,16,512]{2,1,0:T(8,128)(2,1)S(1)}) custom-call(s32[32]{0:T(128)S(1)} %copy-done.5, bf16[1024,256]{1,0:T(8,128)(2,1)S(1)} %copy-done.3, bf16[2,16,96,128]{3,2,1,0:T(8,128)(2,1)S(1)} %copy-done.2, bf16[544,256]{1,0:T(8,128)(2,1)S(1)} %get-tuple-element.22.v_ref, bf16[1024,256]{1,0:T(8,128)(2,1)S(1)} %copy-done), custom_call_target="tpu_custom_call" | custom-call | tf_op jit(solution)/shard_map/finish/pallas_call | solution.py:286
  89.2 38.3 %all_to_all.17.back_ref = bf16[64,16,512]{2,1,0:T(8,128)(2,1)} all-to-all(bf16[64,16,512]{2,1,0:T(8,128)(2,1)S(1)} %get-tuple-element.25), channel_id=1, replica_groups=mesh['dp'=64,'mp'=8] {'dp'}, dimensions={0} | all-to-all | bytes 2097152 | tf_op jit(solution)/shard_map/all_to_all | solution.py:319
  127.5 3.4 %sum_uses.1 = (f32[32,16,256]{2,1,0:T(8,128)}, f32[32,16,256]{2,1,0:T(8,128)}) custom-call(s32[64,1,128]{2,1,0:T(1,128)} %all_to_all.15.want_ref, bf16[64,16,512]{2,1,0:T(8,128)(2,1)} %all_to_all.17.back_ref), custom_call_target="tpu_custom_call" | custom-call | tf_op jit(solution)/shard_map/sum_uses/pallas_call | solution.py:108
  130.9 12.2 %reduce-scatter.2.cloned.1.call-done = bf16[1024,256]{1,0:T(8,128)(2,1)} async-done(((bf16[1024,2048]{1,0:T(8,128)(2,1)}), bf16[1024,256]{1,0:T(8,128)(2,1)}) %reduce-scatter.2.cloned.1.call-update) | async-done | bytes 524304 | tf_op jit(solution)/shard_map/reduce_scatter | solution.py:315
  (3 shorter events, 0.0 us)
Async XLA Ops:
  7.2 59.7 %copy-start = (bf16[1024,256]{1,0:T(8,128)(2,1)S(1)}, bf16[1024,256]{1,0:T(8,128)(2,1)}, u32[]{:S(2)}) copy-start(bf16[1024,256]{1,0:T(8,128)(2,1)} %cot_ref.3) | copy-start | bytes 1572868
  7.2 66.7 %copy-start.1 = (bf16[2048,256]{1,0:T(8,128)(2,1)S(1)}, bf16[2048,256]{1,0:T(8,128)(2,1)}, u32[]{:S(2)}) copy-start(bf16[2048,256]{1,0:T(8,128)(2,1)} %w_ref.1) | copy-start | bytes 3145732
  7.2 66.7 %all-gather.3.cloned.1.call-start = ((), (), s32[]{:S(2)}) async-start(), calls=%async_computation.5 | async-start | bytes 4718592 | tf_op jit(solution)/shard_map/all_gather | solution.py:306
  7.9 135.2 %reduce-scatter.2.cloned.1.call-start = ((), (), s32[]{:S(2)}) async-start(), calls=%async_computation.4 | async-start | bytes 4718592 | tf_op jit(solution)/shard_map/reduce_scatter | solution.py:315
  66.8 0.7 copy-start.4
  73.9 12.3 %copy-start.5 = (s32[32]{0:T(128)S(1)}, s32[32]{0:T(128)}, u32[]{:S(2)}) copy-start(s32[32]{0:T(128)} %get-tuple-element.16.own_ref) | copy-start | bytes 388
  86.1 1.1 copy-start.2
  86.1 1.3 copy-start.3
Sparse Core Ops, SparseCore 0:
  10.1 63.7 all-gather.2
  86.3 56.8 reduce-scatter.1

commit v4 on v3

--- a/solution.py
+++ b/solution.py
@@ -165,7 +165,7 @@
 
     def kernel(
         tok_hbm, w_ref, k_ref, pg_ref, term_hbm, q_hbm, pair_hbm,
-        tok_ref, term_ref, q_ref, pair_ref, qg_ref, in_sem, out_sem, keep_sem,
+        tok_ref, term_ref, q_ref, pair_ref, qg_ref, s_ref, in_sem, out_sem, keep_sem,
     ):
         def load(b):
             rows = slice(b * BLOCK, (b + 1) * BLOCK)
@@ -182,13 +182,18 @@
         inner = key_at == span_of
         first_tile = inner & (key_at > 0)
 
-        def one_tile(t):
-            rows = slice(t * TILE, (t + 1) * TILE)
-            for h in range(heads):
-                cols = slice(h * DH, (h + 1) * DH)
-                k = k_ref[tile_keys_of(t, span_keys), cols]
-                scores = dot_nt(k, q_ref[rows, cols]) * scaling
-                scores = jnp.where(inner if t else first_tile, scores, -jnp.inf)
+        def places(b):
+            for t in range(b * BLOCK // TILE, (b + 1) * BLOCK // TILE):
+                for h in range(heads):
+                    yield t, t * heads + h, slice(t * TILE, (t + 1) * TILE), slice(h * DH, (h + 1) * DH)
+
+        def score(b):
+            for t, i, rows, cols in places(b):
+                s_ref[i] = dot_nt(k_ref[tile_keys_of(t, span_keys), cols], q_ref[rows, cols])
+
+        def weigh(b):
+            for t, i, rows, cols in places(b):
+                scores = jnp.where(inner if t else first_tile, s_ref[i] * scaling, -jnp.inf)
                 top = jnp.max(scores, axis=0, keepdims=True)
                 if t == 0:
                     top = jnp.where(top == -jnp.inf, 0.0, top)
@@ -197,29 +202,53 @@
                 if t == 0:
                     total = jnp.where(total > 0.0, total, 1.0)
                 weights = grown * (1.0 / total)
-                prob_grad = pg_ref[t * heads + h]
+                prob_grad = pg_ref[i]
                 row_delta = jnp.sum(weights * prob_grad, axis=0, keepdims=True)
-                score_grad = (weights * (prob_grad - row_delta)).astype(BF16)
-                pair_ref[0, t * heads + h] = weights.astype(BF16)
-                pair_ref[1, t * heads + h] = score_grad
-                qg_ref[rows, cols] = (dot_tn(score_grad, k) * scaling).astype(BF16)
-
-        for b in range(blocks):
+                pair_ref[0, i] = weights.astype(BF16)
+                pair_ref[1, i] = (weights * (prob_grad - row_delta)).astype(BF16)
+
+        def grad(b):
+            for t, i, rows, cols in places(b):
+                k = k_ref[tile_keys_of(t, span_keys), cols]
+                qg_ref[rows, cols] = (dot_tn(pair_ref[1, i], k) * scaling).astype(BF16)
+
+        def project(b):
             rows = slice(b * BLOCK, (b + 1) * BLOCK)
             load(b).wait()
             x = jnp.concatenate([tok_ref[j, rows, :] for j in range(mp_count)], axis=1)
             q_ref[rows, :] = jnp.dot(x, w_ref[...], preferred_element_type=F32).astype(BF16)
-            for t in range(b * BLOCK // TILE, (b + 1) * BLOCK // TILE):
-                one_tile(t)
-            if b == blocks - 1:
-                keep = [
-                    pltpu.make_async_copy(q_ref, q_hbm, keep_sem.at[0]),
-                    pltpu.make_async_copy(pair_ref, pair_hbm, keep_sem.at[1]),
-                ]
-                for copy in keep:
-                    copy.start()
+
+        def spread(b):
+            rows = slice(b * BLOCK, (b + 1) * BLOCK)
             term_ref[rows, :] = dot_nt(qg_ref[rows, :], w_ref[...]).astype(BF16)
             store(b).start()
+
+        keep = [
+            pltpu.make_async_copy(q_ref, q_hbm, keep_sem.at[0]),
+            pltpu.make_async_copy(pair_ref, pair_hbm, keep_sem.at[1]),
+        ]
+        project(0)
+        project(1)
+        project(2)
+        project(3)
+        score(0)
+        score(1)
+        score(2)
+        score(3)
+        weigh(0)
+        weigh(1)
+        grad(0)
+        grad(1)
+        spread(0)
+        spread(1)
+        weigh(2)
+        weigh(3)
+        grad(2)
+        grad(3)
+        for copy in keep:
+            copy.start()
+        spread(2)
+        spread(3)
         for b in range(blocks):
             store(b).wait()
         for copy in keep:
@@ -240,6 +269,7 @@
             pltpu.VMEM((seq_len, width), BF16),
             pltpu.VMEM((2, *prob_grads.shape), BF16),
             pltpu.VMEM((seq_len, width), BF16),
+            pltpu.VMEM(prob_grads.shape, F32),
             pltpu.SemaphoreType.DMA((blocks,)),
             pltpu.SemaphoreType.DMA((blocks,)),
             pltpu.SemaphoreType.DMA((2,)),

time: 150 us -> 146 us (0.973)
  Pallas kernels: 23.4 us -> 18.6 us
    pallas_call x1, Pallas kernels: 12.2 us -> 7.45 us  [attend(): pl.pallas_call(kernel, out_shape=(pltpu.HBM((seq_len, mp_count * width),...]
  transfers between devices with their start and end apart: 2 -> 2, of which waited for: 2 -> 2; matrix products, arithmetic and copies ran while one was open for 0% -> 0% of each run, Pallas kernels for 7% -> 8%
where the time goes in v4:
time: 146 us; the launch traced here: 145 us
  blocking collectives  92.2 us (63%)
  Pallas kernels  18.6 us (13%)
  waiting for transfers between devices  18.4 us (13%)
  between operations  14.1 us (10%)
  local copies, waits for them, and re-layouts  1.9 us (1%)
    all_to_all x1, blocking collectives, body(): back = lax.all_to_all(uses, 'dp', split_axis=0, concat_axis=0, tiled=True)  38.3 us
    all_to_all x1, blocking collectives, body(): got = lax.all_to_all(picked, 'dp', split_axis=0, concat_axis=0, tiled=True)  32.8 us
    all_to_all x1, blocking collectives, body(): lax.all_to_all(request, 'dp', split_axis=0, concat_axis=0, tiled=True)  21.2 us
    reduce_scatter x1, waiting for transfers between devices, body(): input_grad = lax.psum_scatter(terms, 'mp', scatter_dimension=1, tiled=True)  12.3 us
    pallas_call x1, Pallas kernels, attend(): pl.pallas_call(kernel, out_shape=(pltpu.HBM((seq_len, mp_count * width),...  7.45 us
    all_gather x1, waiting for transfers between devices, body(): gathered = lax.all_gather(tokens, 'mp', axis=0, tiled=False)  5.38 us
    pallas_call x1, Pallas kernels, sum_uses(): pl.pallas_call(kernel, out_shape=(out, out), in_specs=[SMEM, VMEM], out_s...  3.37 us
  transfers between devices with their start and end apart: 2, of which 2 were waited for; matrix products, arithmetic and copies ran while one was open for 0% of the time, Pallas kernels for 8%

profile of v4, /device:TPU:1, one launch (start us, length us, event | category | flops | bytes accessed | tf_op | source)
XLA Modules:
  0.0 145.2 jit_solution(16674965677466209823)
XLA Ops:
  7.2 0.0 copy-start
  7.2 0.0 copy-start.1
  7.2 0.0 all-gather.3.cloned.1.call-start
  7.2 0.7 all-gather.3.cloned.1.call-update
  7.9 0.0 reduce-scatter.2.cloned.1.call-start
  8.0 2.5 %request_rows.1 = (s32[64,1,128]{2,1,0:T(1,128)}, s32[32]{0:T(128)}) custom-call(s32[2,16]{1,0:T(2,128)} %bitcast.3, s32[2048]{0:T(1024)} %slot_ref.1), custom_call_target="tpu_custom_call" | custom-call | tf_op jit(solution)/shard_map/request_rows/pallas_call | solution.py:52
  10.5 21.2 %all_to_all.15.want_ref = s32[64,1,128]{2,1,0:T(1,128)} all-to-all(s32[64,1,128]{2,1,0:T(1,128)} %get-tuple-element.17), channel_id=1, replica_groups=mesh['dp'=64,'mp'=8] {'dp'}, dimensions={0} | all-to-all | bytes 65536 | tf_op jit(solution)/shard_map/all_to_all | solution.py:338
  31.7 2.4 %pick_rows.1 = bf16[64,16,512]{2,1,0:T(8,128)(2,1)} custom-call(s32[64,1,128]{2,1,0:T(1,128)} %all_to_all.15.want_ref, bf16[32,16,256]{2,1,0:T(8,128)(2,1)} %key_ref.1, bf16[32,16,256]{2,1,0:T(8,128)(2,1)} %value_ref.1), custom_call_target="tpu_custom_call" | custom-call | tf_op jit(solution)/shard_map/pick_rows/pallas_call | solution.py:77
  34.0 32.8 %all_to_all.16.got_ref = bf16[64,16,512]{2,1,0:T(8,128)(2,1)S(1)} all-to-all(bf16[64,16,512]{2,1,0:T(8,128)(2,1)} %pick_rows.1), channel_id=1, replica_groups=mesh['dp'=64,'mp'=8] {'dp'}, dimensions={0} | all-to-all | bytes 2097152 | tf_op jit(solution)/shard_map/all_to_all | solution.py:340
  66.8 0.0 copy-done
  66.8 0.7 copy-done.4
  67.5 1.0 prepare.1
  68.5 5.4 %all-gather.3.cloned.1.call-done = bf16[8192,256]{1,0:T(8,128)(2,1)} async-done(((bf16[1024,256]{1,0:T(8,128)(2,1)}), bf16[8192,256]{1,0:T(8,128)(2,1)}) %all-gather.3.cloned.1.call-update) | async-done | bytes 4194320 | tf_op jit(solution)/shard_map/all_gather | solution.py:336
  73.9 0.0 copy-done.1
  73.9 7.4 %attend.1 = (bf16[1024,2048]{1,0:T(8,128)(2,1)}, bf16[1024,256]{1,0:T(8,128)(2,1)}, bf16[2,16,96,128]{3,2,1,0:T(8,128)(2,1)}) custom-call(bf16[8,1024,256]{2,1,0:T(8,128)(2,1)} %bitcast.2, bf16[2048,256]{1,0:T(8,128)(2,1)S(1)} %copy-done.1, bf16[544,256]{1,0:T(8,128)(2,1)S(1)} %get-tuple-element.18.k_ref, f32[16,96,128]{2,1,0:T(8,128)S(1)} %get-tuple-element.19.pg_ref), custom_call_target="tpu_custom_call" | custom-call | tf_op jit(solution)/shard_map/attend/pallas_call | solution.py:257
  81.3 0.0 copy-start.2
  81.3 0.0 copy-start.3
  81.4 0.0 reduce-scatter.2.cloned.1.call-update
  81.4 1.1 copy-done.2
  82.5 0.1 copy-done.3
  82.6 1.9 %finish.1 = (bf16[1024,256]{1,0:T(8,128)(2,1)}, bf16[64,16,512]{2,1,0:T(8,128)(2,1)S(1)}) custom-call(s32[32]{0:T(128)S(1)} %copy-done.5, bf16[1024,256]{1,0:T(8,128)(2,1)S(1)} %copy-done.3, bf16[2,16,96,128]{3,2,1,0:T(8,128)(2,1)S(1)} %copy-done.2, bf16[544,256]{1,0:T(8,128)(2,1)S(1)} %get-tuple-element.22.v_ref, bf16[1024,256]{1,0:T(8,128)(2,1)S(1)} %copy-done), custom_call_target="tpu_custom_call" | custom-call | tf_op jit(solution)/shard_map/finish/pallas_call | solution.py:316
  84.5 38.3 %all_to_all.17.back_ref = bf16[64,16,512]{2,1,0:T(8,128)(2,1)} all-to-all(bf16[64,16,512]{2,1,0:T(8,128)(2,1)S(1)} %get-tuple-element.25), channel_id=1, replica_groups=mesh['dp'=64,'mp'=8] {'dp'}, dimensions={0} | all-to-all | bytes 2097152 | tf_op jit(solution)/shard_map/all_to_all | solution.py:349
  122.8 3.4 %sum_uses.1 = (f32[32,16,256]{2,1,0:T(8,128)}, f32[32,16,256]{2,1,0:T(8,128)}) custom-call(s32[64,1,128]{2,1,0:T(1,128)} %all_to_all.15.want_ref, bf16[64,16,512]{2,1,0:T(8,128)(2,1)} %all_to_all.17.back_ref), custom_call_target="tpu_custom_call" | custom-call | tf_op jit(solution)/shard_map/sum_uses/pallas_call | solution.py:108
  126.1 12.3 %reduce-scatter.2.cloned.1.call-done = bf16[1024,256]{1,0:T(8,128)(2,1)} async-done(((bf16[1024,2048]{1,0:T(8,128)(2,1)}), bf16[1024,256]{1,0:T(8,128)(2,1)}) %reduce-scatter.2.cloned.1.call-update) | async-done | bytes 524304 | tf_op jit(solution)/shard_map/reduce_scatter | solution.py:345
  (3 shorter events, 0.0 us)
Async XLA Ops:
  7.2 59.7 %copy-start = (bf16[1024,256]{1,0:T(8,128)(2,1)S(1)}, bf16[1024,256]{1,0:T(8,128)(2,1)}, u32[]{:S(2)}) copy-start(bf16[1024,256]{1,0:T(8,128)(2,1)} %cot_ref.3) | copy-start | bytes 1572868
  7.2 66.7 %copy-start.1 = (bf16[2048,256]{1,0:T(8,128)(2,1)S(1)}, bf16[2048,256]{1,0:T(8,128)(2,1)}, u32[]{:S(2)}) copy-start(bf16[2048,256]{1,0:T(8,128)(2,1)} %w_ref.1) | copy-start | bytes 3145732
  7.2 66.7 %all-gather.3.cloned.1.call-start = ((), (), s32[]{:S(2)}) async-start(), calls=%async_computation.5 | async-start | bytes 4718592 | tf_op jit(solution)/shard_map/all_gather | solution.py:336
  7.9 130.5 %reduce-scatter.2.cloned.1.call-start = ((), (), s32[]{:S(2)}) async-start(), calls=%async_computation.4 | async-start | bytes 4718592 | tf_op jit(solution)/shard_map/reduce_scatter | solution.py:345
  66.8 0.7 copy-start.4
  73.9 7.5 %copy-start.5 = (s32[32]{0:T(128)S(1)}, s32[32]{0:T(128)}, u32[]{:S(2)}) copy-start(s32[32]{0:T(128)} %get-tuple-element.16.own_ref) | copy-start | bytes 388
  81.3 1.1 copy-start.2
  81.3 1.3 copy-start.3
Sparse Core Ops, SparseCore 0:
  10.1 63.7 all-gather.2
  81.5 56.8 reduce-scatter.1

commit v5 on v3

--- a/solution.py
+++ b/solution.py
@@ -156,128 +156,142 @@
     )(owners, cotangent, got)
 
 
+def tile_places(seq_len, heads, low, high):
+    for t in range(low // TILE, high // TILE):
+        for h in range(heads):
+            yield t, t * heads + h, slice(t * TILE, (t + 1) * TILE), slice(h * DH, (h + 1) * DH)
+
+
+def attends(tile_keys, span_keys):
+    key_at = lax.broadcasted_iota(jnp.int32, (tile_keys, TILE), 0) // span_keys
+    span_of = (lax.broadcasted_iota(jnp.int32, (tile_keys, TILE), 1) + 1) // SPAN
+    inner = key_at == span_of
+    return inner, inner & (key_at > 0)
+
+
+def weigh(products, prob_grad, masks, t):
+    scores = jnp.where(masks[0] if t else masks[1], products * (1.0 / math.sqrt(DH)), -jnp.inf)
+    top = jnp.max(scores, axis=0, keepdims=True)
+    if t == 0:
+        top = jnp.where(top == -jnp.inf, 0.0, top)
+    grown = jnp.exp(scores - top)
+    total = jnp.sum(grown, axis=0, keepdims=True)
+    if t == 0:
+        total = jnp.where(total > 0.0, total, 1.0)
+    weights = grown * (1.0 / total)
+    row_delta = jnp.sum(weights * prob_grad, axis=0, keepdims=True)
+    return weights.astype(BF16), (weights * (prob_grad - row_delta)).astype(BF16)
+
+
 def attend(tokens, q_weight, keys, prob_grads, seq_len, span_keys):
-    mp_count, _, width = tokens.shape
+    mp_count, given, width = tokens.shape
     heads = width // DH
     blocks = seq_len // BLOCK
     tile_keys = prob_grads.shape[1]
     scaling = 1.0 / math.sqrt(DH)
+    skip = seq_len - given
+    half = seq_len // 2
 
     def kernel(
-        tok_hbm, w_ref, k_ref, pg_ref, term_hbm, q_hbm, pair_hbm,
-        tok_ref, term_ref, q_ref, pair_ref, qg_ref, in_sem, out_sem, keep_sem,
+        tok_hbm, w_ref, k_ref, pg_ref, term_hbm, q_hbm,
+        tok_ref, term_ref, q_ref, sg_ref, qg_ref, s_ref, in_sem, out_sem, keep_sem,
     ):
-        def load(b):
-            rows = slice(b * BLOCK, (b + 1) * BLOCK)
-            return pltpu.make_async_copy(tok_hbm.at[:, rows, :], tok_ref.at[:, rows, :], in_sem.at[b])
+        def load(i):
+            low, high = (half, seq_len) if i else (skip, half)
+            source = tok_hbm.at[:, low - skip : high - skip, :]
+            return pltpu.make_async_copy(source, tok_ref.at[:, low:high, :], in_sem.at[i])
 
         def store(b):
             rows = slice(b * BLOCK, (b + 1) * BLOCK)
             return pltpu.make_async_copy(term_ref.at[rows, :], term_hbm.at[rows, :], out_sem.at[b])
 
+        load(0).start()
+        load(1).start()
+        keep = pltpu.make_async_copy(q_ref, q_hbm, keep_sem)
+        masks = attends(tile_keys, span_keys)
+        if skip:
+            q_ref[:skip, :] = jnp.zeros((skip, width), BF16)
+        load(0).wait()
         for b in range(blocks):
-            load(b).start()
-        key_at = lax.broadcasted_iota(jnp.int32, (tile_keys, TILE), 0) // span_keys
-        span_of = (lax.broadcasted_iota(jnp.int32, (tile_keys, TILE), 1) + 1) // SPAN
-        inner = key_at == span_of
-        first_tile = inner & (key_at > 0)
-
-        def one_tile(t):
-            rows = slice(t * TILE, (t + 1) * TILE)
-            for h in range(heads):
-                cols = slice(h * DH, (h + 1) * DH)
-                k = k_ref[tile_keys_of(t, span_keys), cols]
-                scores = dot_nt(k, q_ref[rows, cols]) * scaling
-                scores = jnp.where(inner if t else first_tile, scores, -jnp.inf)
-                top = jnp.max(scores, axis=0, keepdims=True)
-                if t == 0:
-                    top = jnp.where(top == -jnp.inf, 0.0, top)
-                grown = jnp.exp(scores - top)
-                total = jnp.sum(grown, axis=0, keepdims=True)
-                if t == 0:
-                    total = jnp.where(total > 0.0, total, 1.0)
-                weights = grown * (1.0 / total)
-                prob_grad = pg_ref[t * heads + h]
-                row_delta = jnp.sum(weights * prob_grad, axis=0, keepdims=True)
-                score_grad = (weights * (prob_grad - row_delta)).astype(BF16)
-                pair_ref[0, t * heads + h] = weights.astype(BF16)
-                pair_ref[1, t * heads + h] = score_grad
-                qg_ref[rows, cols] = (dot_tn(score_grad, k) * scaling).astype(BF16)
-
-        for b in range(blocks):
-            rows = slice(b * BLOCK, (b + 1) * BLOCK)
-            load(b).wait()
+            if b * BLOCK == half:
+                load(1).wait()
+            rows = slice(max(b * BLOCK, skip), (b + 1) * BLOCK)
             x = jnp.concatenate([tok_ref[j, rows, :] for j in range(mp_count)], axis=1)
             q_ref[rows, :] = jnp.dot(x, w_ref[...], preferred_element_type=F32).astype(BF16)
-            for t in range(b * BLOCK // TILE, (b + 1) * BLOCK // TILE):
-                one_tile(t)
-            if b == blocks - 1:
-                keep = [
-                    pltpu.make_async_copy(q_ref, q_hbm, keep_sem.at[0]),
-                    pltpu.make_async_copy(pair_ref, pair_hbm, keep_sem.at[1]),
-                ]
-                for copy in keep:
-                    copy.start()
-            term_ref[rows, :] = dot_nt(qg_ref[rows, :], w_ref[...]).astype(BF16)
-            store(b).start()
+        keep.start()
+        for t, i, rows, cols in tile_places(seq_len, heads, 0, seq_len):
+            s_ref[i] = dot_nt(k_ref[tile_keys_of(t, span_keys), cols], q_ref[rows, cols])
+        for low in (0, half):
+            for t, i, rows, cols in tile_places(seq_len, heads, low, low + half):
+                _, sg_ref[i] = weigh(s_ref[i], pg_ref[i], masks, t)
+            for t, i, rows, cols in tile_places(seq_len, heads, low, low + half):
+                k = k_ref[tile_keys_of(t, span_keys), cols]
+                qg_ref[rows, cols] = (dot_tn(sg_ref[i], k) * scaling).astype(BF16)
+            for b in range(low // BLOCK, (low + half) // BLOCK):
+                rows = slice(b * BLOCK, (b + 1) * BLOCK)
+                term_ref[rows, :] = dot_nt(qg_ref[rows, :], w_ref[...]).astype(BF16)
+                store(b).start()
         for b in range(blocks):
             store(b).wait()
-        for copy in keep:
-            copy.wait()
+        keep.wait()
 
     return pl.pallas_call(
         kernel,
         out_shape=(
             pltpu.HBM((seq_len, mp_count * width), BF16),
             pltpu.HBM((seq_len, width), BF16),
-            pltpu.HBM((2, *prob_grads.shape), BF16),
         ),
         in_specs=[HBM, VMEM, VMEM, VMEM],
-        out_specs=(HBM, HBM, HBM),
+        out_specs=(HBM, HBM),
         scratch_shapes=[
             pltpu.VMEM((mp_count, seq_len, width), BF16),
             pltpu.VMEM((seq_len, mp_count * width), BF16),
             pltpu.VMEM((seq_len, width), BF16),
-            pltpu.VMEM((2, *prob_grads.shape), BF16),
+            pltpu.VMEM(prob_grads.shape, BF16),
             pltpu.VMEM((seq_len, width), BF16),
+            pltpu.VMEM(prob_grads.shape, F32),
+            pltpu.SemaphoreType.DMA((2,)),
             pltpu.SemaphoreType.DMA((blocks,)),
-            pltpu.SemaphoreType.DMA((blocks,)),
-            pltpu.SemaphoreType.DMA((2,)),
+            pltpu.SemaphoreType.DMA(()),
         ],
         compiler_params=pltpu.CompilerParams(vmem_limit_bytes=24 * 1024 * 1024),
         name="attend",
     )(pltpu.with_memory_space_constraint(tokens, pltpu.HBM), q_weight, keys, prob_grads)
 
 
-def finish(owners, queries, pairs, values, cotangent, dp_count):
+def finish(owners, queries, keys, values, prob_grads, cotangent, dp_count):
     seq_len, width = cotangent.shape
     heads = width // DH
-    tiles = seq_len // TILE
     picks = owners.shape[0]
     span_keys = values.shape[0] // (seq_len // SPAN + 1)
     nei = span_keys // NEIGH
+    tile_keys = prob_grads.shape[1]
     scaling = 1.0 / math.sqrt(DH)
 
-    def kernel(own_ref, q_ref, pair_ref, v_ref, cot_ref, att_ref, use_ref, ku_ref, vu_ref):
+    def kernel(
+        own_ref, q_ref, k_ref, v_ref, pg_ref, cot_ref, att_ref, use_ref,
+        s_ref, p_ref, sg_ref, ku_ref, vu_ref,
+    ):
         use_ref[...] = jnp.zeros_like(use_ref)
-        for t in range(tiles):
-            rows = slice(t * TILE, (t + 1) * TILE)
+        masks = attends(tile_keys, span_keys)
+        for t, i, rows, cols in tile_places(seq_len, heads, 0, seq_len):
+            s_ref[i] = dot_nt(k_ref[tile_keys_of(t, span_keys), cols], q_ref[rows, cols])
+        for t, i, rows, cols in tile_places(seq_len, heads, 0, seq_len):
+            p_ref[i], sg_ref[i] = weigh(s_ref[i], pg_ref[i], masks, t)
+        for t, i, rows, cols in tile_places(seq_len, heads, 0, seq_len):
             keys_at = tile_keys_of(t, span_keys)
             start, mid, end = keys_at.start, keys_at.start + span_keys, keys_at.stop
-            for h in range(heads):
-                cols = slice(h * DH, (h + 1) * DH)
-                p = pair_ref[0, t * heads + h]
-                key_use = jnp.dot(pair_ref[1, t * heads + h], q_ref[rows, cols], preferred_element_type=F32)
-                value_use = jnp.dot(p, cot_ref[rows, cols], preferred_element_type=F32)
-                att_ref[rows, cols] = dot_tn(p, v_ref[keys_at, cols]).astype(BF16)
-                if t == 0:
-                    ku_ref[start:mid, cols] = key_use[:span_keys]
-                    vu_ref[start:mid, cols] = value_use[:span_keys]
-                else:
-                    ku_ref[start:mid, cols] += key_use[:span_keys]
-                    vu_ref[start:mid, cols] += value_use[:span_keys]
-                ku_ref[mid:end, cols] = key_use[span_keys:]
-                vu_ref[mid:end, cols] = value_use[span_keys:]
+            key_use = jnp.dot(sg_ref[i], q_ref[rows, cols], preferred_element_type=F32)
+            value_use = jnp.dot(p_ref[i], cot_ref[rows, cols], preferred_element_type=F32)
+            att_ref[rows, cols] = dot_tn(p_ref[i], v_ref[keys_at, cols]).astype(BF16)
+            if t == 0:
+                ku_ref[start:mid, cols] = key_use[:span_keys]
+                vu_ref[start:mid, cols] = value_use[:span_keys]
+            else:
+                ku_ref[start:mid, cols] += key_use[:span_keys]
+                vu_ref[start:mid, cols] += value_use[:span_keys]
+            ku_ref[mid:end, cols] = key_use[span_keys:]
+            vu_ref[mid:end, cols] = value_use[span_keys:]
         for n in range(picks):
             at = span_keys + n * nei
             use_ref[own_ref[n], :, :width] = (ku_ref[at : at + nei, :] * scaling).astype(BF16)
@@ -289,12 +303,18 @@
             jax.ShapeDtypeStruct((seq_len, width), BF16),
             jax.ShapeDtypeStruct((dp_count, nei, 2 * width), BF16),
         ),
-        in_specs=[SMEM] + [VMEM] * 4,
+        in_specs=[SMEM] + [VMEM] * 5,
         out_specs=(VMEM, VMEM),
-        scratch_shapes=[pltpu.VMEM(values.shape, F32), pltpu.VMEM(values.shape, F32)],
-        compiler_params=pltpu.CompilerParams(vmem_limit_bytes=16 * 1024 * 1024),
+        scratch_shapes=[
+            pltpu.VMEM(prob_grads.shape, F32),
+            pltpu.VMEM(prob_grads.shape, BF16),
+            pltpu.VMEM(prob_grads.shape, BF16),
+            pltpu.VMEM(values.shape, F32),
+            pltpu.VMEM(values.shape, F32),
+        ],
+        compiler_params=pltpu.CompilerParams(vmem_limit_bytes=20 * 1024 * 1024),
         name="finish",
-    )(owners, queries, pairs, values, cotangent)
+    )(owners, queries, keys, values, prob_grads, cotangent)
 
 
 def body(
@@ -303,18 +323,19 @@
     dp_count = lax.axis_size("dp")
     seq_len = tokens.shape[0]
     snip_count, nei, _ = snippet_keys.shape
-    gathered = lax.all_gather(tokens, "mp", axis=0, tiled=False)
+    skip = (SPAN - 1) // 16 * 16
+    gathered = lax.all_gather(tokens[skip:], "mp", axis=0, tiled=False)
     request, owners = request_rows(neighbour_ids.T, snippet_slot, snip_count, dp_count)
     wanted = lax.all_to_all(request, "dp", split_axis=0, concat_axis=0, tiled=True)
     picked = pick_rows(wanted, snippet_keys, snippet_values)
     got = lax.all_to_all(picked, "dp", split_axis=0, concat_axis=0, tiled=True)
     values, keys, prob_grads = prepare(owners, out_cotangent, got)
-    terms, queries, pairs = attend(
+    terms, queries = attend(
         gathered, q_weight, keys, prob_grads, seq_len, NEIGH * nei
     )
     input_grad = lax.psum_scatter(terms, "mp", scatter_dimension=1, tiled=True)
     attended, uses = finish(
-        owners, queries, pairs, values, out_cotangent, dp_count
+        owners, queries, keys, values, prob_grads, out_cotangent, dp_count
     )
     back = lax.all_to_all(uses, "dp", split_axis=0, concat_axis=0, tiled=True)
     key_grad, value_grad = sum_uses(wanted, back, snip_count)

time: 150 us -> 143 us (0.953)
  Pallas kernels: 23.4 us -> 17.9 us
  waiting for transfers between devices: 18.3 us -> 14.8 us
  local copies, waits for them, and re-layouts: 1.9 us -> 3.62 us
    pallas_call x1, Pallas kernels: 12.2 us -> 6.18 us  [attend(): pl.pallas_call(kernel, out_shape=(pltpu.HBM((seq_len, mp_count * width),...]
    all_gather x1, waiting for transfers between devices: 5.37 us -> 2.83 us  [body(): gathered = lax.all_gather(tokens[skip:], 'mp', axis=0, tiled=False)]
    slice x0 -> x1, local copies, waits for them, and re-layouts: none -> 1.95 us  [body(): gathered = lax.all_gather(tokens[skip:], 'mp', axis=0, tiled=False)]
  transfers between devices with their start and end apart: 2 -> 2, of which waited for: 2 -> 2; matrix products, arithmetic and copies ran while one was open for 0% -> 0% of each run, Pallas kernels for 7% -> 8%
where the time goes in v5:
time: 143 us
  blocking collectives  92.2 us (64%)
  Pallas kernels  17.9 us (13%)
  waiting for transfers between devices  14.8 us (10%)
  between operations  14.1 us (10%)
  local copies, waits for them, and re-layouts  3.62 us (3%)
    all_to_all x1, blocking collectives, body(): back = lax.all_to_all(uses, 'dp', split_axis=0, concat_axis=0, tiled=True)  38.3 us
    all_to_all x1, blocking collectives, body(): got = lax.all_to_all(picked, 'dp', split_axis=0, concat_axis=0, tiled=True)  32.8 us
    all_to_all x1, blocking collectives, body(): lax.all_to_all(request, 'dp', split_axis=0, concat_axis=0, tiled=True)  21.2 us
    reduce_scatter x1, waiting for transfers between devices, body(): input_grad = lax.psum_scatter(terms, 'mp', scatter_dimension=1, tiled=True)  11.9 us
    pallas_call x1, Pallas kernels, attend(): pl.pallas_call(kernel, out_shape=(pltpu.HBM((seq_len, mp_count * width),...  6.18 us
    pallas_call x1, Pallas kernels, sum_uses(): pl.pallas_call(kernel, out_shape=(out, out), in_specs=[SMEM, VMEM], out_s...  3.34 us
  transfers between devices with their start and end apart: 2, of which 2 were waited for; matrix products, arithmetic and copies ran while one was open for 0% of the time, Pallas kernels for 8%

profile of v5, /device:TPU:1, one launch (start us, length us, event | category | flops | bytes accessed | tf_op | source)
XLA Modules:
  0.0 142.7 jit_solution(10661386939494384956)
XLA Ops:
  7.2 0.0 copy-start
  7.2 0.0 copy-start.1
  7.2 0.0 all-gather.3.cloned.1.call-start
  7.2 2.0 %slice.3 = bf16[976,256]{1,0:T(8,128)(2,1)} slice(bf16[1024,256]{1,0:T(8,128)(2,1)} %param.7), slice={[48:1024], [0:256]} | slice | bytes 999424 | tf_op jit(solution)/shard_map/slice | solution.py:327
  9.2 0.0 all-gather.3.cloned.1.call-update
  9.2 0.0 reduce-scatter.2.cloned.1.call-start
  9.3 2.5 %request_rows.1 = (s32[64,1,128]{2,1,0:T(1,128)}, s32[32]{0:T(128)}) custom-call(s32[2,16]{1,0:T(2,128)} %bitcast.3, s32[2048]{0:T(1024)} %slot_ref.1), custom_call_target="tpu_custom_call" | custom-call | tf_op jit(solution)/shard_map/request_rows/pallas_call | solution.py:52
  11.8 21.2 %all_to_all.15.want_ref = s32[64,1,128]{2,1,0:T(1,128)} all-to-all(s32[64,1,128]{2,1,0:T(1,128)} %get-tuple-element.16), channel_id=1, replica_groups=mesh['dp'=64,'mp'=8] {'dp'}, dimensions={0} | all-to-all | bytes 65536 | tf_op jit(solution)/shard_map/all_to_all | solution.py:329
  32.9 2.4 %pick_rows.1 = bf16[64,16,512]{2,1,0:T(8,128)(2,1)} custom-call(s32[64,1,128]{2,1,0:T(1,128)} %all_to_all.15.want_ref, bf16[32,16,256]{2,1,0:T(8,128)(2,1)} %key_ref.1, bf16[32,16,256]{2,1,0:T(8,128)(2,1)} %value_ref.1), custom_call_target="tpu_custom_call" | custom-call | tf_op jit(solution)/shard_map/pick_rows/pallas_call | solution.py:77
  35.3 32.8 %all_to_all.16.got_ref = bf16[64,16,512]{2,1,0:T(8,128)(2,1)S(1)} all-to-all(bf16[64,16,512]{2,1,0:T(8,128)(2,1)} %pick_rows.1), channel_id=1, replica_groups=mesh['dp'=64,'mp'=8] {'dp'}, dimensions={0} | all-to-all | bytes 2097152 | tf_op jit(solution)/shard_map/all_to_all | solution.py:331
  68.1 0.0 copy-done
  68.1 0.7 copy-done.3
  68.8 1.0 prepare.1
  69.8 2.8 %all-gather.3.cloned.1.call-done = bf16[7808,256]{1,0:T(8,128)(2,1)} async-done(((bf16[976,256]{1,0:T(8,128)(2,1)}), bf16[7808,256]{1,0:T(8,128)(2,1)}) %all-gather.3.cloned.1.call-update) | async-done | bytes 3997712 | tf_op jit(solution)/shard_map/all_gather | solution.py:327
  72.6 0.0 copy-done.1
  72.6 6.2 %attend.1 = (bf16[1024,2048]{1,0:T(8,128)(2,1)}, bf16[1024,256]{1,0:T(8,128)(2,1)}) custom-call(bf16[8,976,256]{2,1,0:T(8,128)(2,1)} %bitcast.2, bf16[2048,256]{1,0:T(8,128)(2,1)S(1)} %copy-done.1, bf16[544,256]{1,0:T(8,128)(2,1)S(1)} %get-tuple-element.17.k_ref, f32[16,96,128]{2,1,0:T(8,128)S(1)} %get-tuple-element.18.pg_ref), custom_call_target="tpu_custom_call" | custom-call | tf_op jit(solution)/shard_map/attend/pallas_call | solution.py:238
  78.8 0.0 copy-start.2
  78.8 0.0 reduce-scatter.2.cloned.1.call-update
  78.8 0.0 copy-done.4
  78.8 1.0 copy-done.2
  79.8 2.5 %finish.1 = (bf16[1024,256]{1,0:T(8,128)(2,1)}, bf16[64,16,512]{2,1,0:T(8,128)(2,1)S(1)}) custom-call(s32[32]{0:T(128)S(1)} %copy-done.4, bf16[1024,256]{1,0:T(8,128)(2,1)S(1)} %copy-done.2, bf16[544,256]{1,0:T(8,128)(2,1)S(1)} %get-tuple-element.17.k_ref, bf16[544,256]{1,0:T(8,128)(2,1)S(1)} %get-tuple-element.20.v_ref, ...), custom_call_target="tpu_custom_call" | custom-call | tf_op jit(solution)/shard_map/finish/pallas_call | solution.py:300
  82.3 38.3 %all_to_all.17.back_ref = bf16[64,16,512]{2,1,0:T(8,128)(2,1)} all-to-all(bf16[64,16,512]{2,1,0:T(8,128)(2,1)S(1)} %get-tuple-element.23), channel_id=1, replica_groups=mesh['dp'=64,'mp'=8] {'dp'}, dimensions={0} | all-to-all | bytes 2097152 | tf_op jit(solution)/shard_map/all_to_all | solution.py:340
  120.6 3.3 %sum_uses.1 = (f32[32,16,256]{2,1,0:T(8,128)}, f32[32,16,256]{2,1,0:T(8,128)}) custom-call(s32[64,1,128]{2,1,0:T(1,128)} %all_to_all.15.want_ref, bf16[64,16,512]{2,1,0:T(8,128)(2,1)} %all_to_all.17.back_ref), custom_call_target="tpu_custom_call" | custom-call | tf_op jit(solution)/shard_map/sum_uses/pallas_call | solution.py:108
  123.9 11.9 %reduce-scatter.2.cloned.1.call-done = bf16[1024,256]{1,0:T(8,128)(2,1)} async-done(((bf16[1024,2048]{1,0:T(8,128)(2,1)}), bf16[1024,256]{1,0:T(8,128)(2,1)}) %reduce-scatter.2.cloned.1.call-update) | async-done | bytes 524304 | tf_op jit(solution)/shard_map/reduce_scatter | solution.py:336
  (2 shorter events, 0.0 us)
Async XLA Ops:
  7.2 60.9 %copy-start = (bf16[1024,256]{1,0:T(8,128)(2,1)S(1)}, bf16[1024,256]{1,0:T(8,128)(2,1)}, u32[]{:S(2)}) copy-start(bf16[1024,256]{1,0:T(8,128)(2,1)} %cot_ref.3) | copy-start | bytes 1572868
  7.2 65.4 %copy-start.1 = (bf16[2048,256]{1,0:T(8,128)(2,1)S(1)}, bf16[2048,256]{1,0:T(8,128)(2,1)}, u32[]{:S(2)}) copy-start(bf16[2048,256]{1,0:T(8,128)(2,1)} %w_ref.1) | copy-start | bytes 3145732
  7.2 65.4 %all-gather.3.cloned.1.call-start = ((), (), s32[]{:S(2)}) async-start(), calls=%async_computation.5 | async-start | bytes 4497408 | tf_op jit(solution)/shard_map/all_gather | solution.py:327
  9.2 126.6 %reduce-scatter.2.cloned.1.call-start = ((), (), s32[]{:S(2)}) async-start(), calls=%async_computation.4 | async-start | bytes 4718592 | tf_op jit(solution)/shard_map/reduce_scatter | solution.py:336
  68.1 0.7 copy-start.3
  72.6 6.2 %copy-start.4 = (s32[32]{0:T(128)S(1)}, s32[32]{0:T(128)}, u32[]{:S(2)}) copy-start(s32[32]{0:T(128)} %get-tuple-element.15.own_ref) | copy-start | bytes 388
  78.8 1.0 copy-start.2
Sparse Core Ops, SparseCore 0:
  10.7 61.8 all-gather.2
  79.0 56.8 reduce-scatter.1

commit v6 on v5

--- a/solution.py
+++ b/solution.py
@@ -37,7 +37,7 @@
             req_ref[i, 0, 0] = 0
             return c
 
-        lax.fori_loop(0, dp_count, clear, 0)
+        lax.fori_loop(0, dp_count, clear, 0, unroll=16)
 
         def step(i, c):
             for n in range(NEIGH):
@@ -47,7 +47,7 @@
                 own_ref[i * NEIGH + n] = owner
             return c
 
-        lax.fori_loop(0, spans, step, 0)
+        lax.fori_loop(0, spans, step, 0, unroll=4)
 
     return pl.pallas_call(
         kernel,
@@ -76,7 +76,7 @@
 
     return pl.pallas_call(
         kernel,
-        out_shape=jax.ShapeDtypeStruct((dp_count, nei, 2 * width), keys.dtype),
+        out_shape=pltpu.VMEM((dp_count, nei, 2 * width), keys.dtype),
         in_specs=[SMEM, VMEM, VMEM],
         out_specs=VMEM,
         name="pick_rows",
@@ -153,7 +153,7 @@
         out_specs=(VMEM, VMEM, VMEM),
         compiler_params=pltpu.CompilerParams(vmem_limit_bytes=16 * 1024 * 1024),
         name="prepare",
-    )(owners, cotangent, got)
+    )(pltpu.with_memory_space_constraint(owners, pltpu.HBM), cotangent, got)
 
 
 def tile_places(seq_len, heads, low, high):
@@ -184,12 +184,12 @@
 
 
 def attend(tokens, q_weight, keys, prob_grads, seq_len, span_keys):
-    mp_count, given, width = tokens.shape
+    mp_count, _, width = tokens.shape
     heads = width // DH
     blocks = seq_len // BLOCK
     tile_keys = prob_grads.shape[1]
     scaling = 1.0 / math.sqrt(DH)
-    skip = seq_len - given
+    skip = (SPAN - 1) // 16 * 16
     half = seq_len // 2
 
     def kernel(
@@ -198,7 +198,7 @@
     ):
         def load(i):
             low, high = (half, seq_len) if i else (skip, half)
-            source = tok_hbm.at[:, low - skip : high - skip, :]
+            source = tok_hbm.at[:, low:high, :]
             return pltpu.make_async_copy(source, tok_ref.at[:, low:high, :], in_sem.at[i])
 
         def store(b):
@@ -209,8 +209,7 @@
         load(1).start()
         keep = pltpu.make_async_copy(q_ref, q_hbm, keep_sem)
         masks = attends(tile_keys, span_keys)
-        if skip:
-            q_ref[:skip, :] = jnp.zeros((skip, width), BF16)
+        q_ref[:skip, :] = jnp.zeros((skip, width), BF16)
         load(0).wait()
         for b in range(blocks):
             if b * BLOCK == half:
@@ -323,8 +322,7 @@
     dp_count = lax.axis_size("dp")
     seq_len = tokens.shape[0]
     snip_count, nei, _ = snippet_keys.shape
-    skip = (SPAN - 1) // 16 * 16
-    gathered = lax.all_gather(tokens[skip:], "mp", axis=0, tiled=False)
+    gathered = lax.all_gather(tokens, "mp", axis=0, tiled=False)
     request, owners = request_rows(neighbour_ids.T, snippet_slot, snip_count, dp_count)
     wanted = lax.all_to_all(request, "dp", split_axis=0, concat_axis=0, tiled=True)
     picked = pick_rows(wanted, snippet_keys, snippet_values)

time: 143 us -> 144 us (level)
  waiting for transfers between devices: 14.8 us -> 20.6 us
  local copies, waits for them, and re-layouts: 3.62 us -> 1.01 us
    all_gather x1, waiting for transfers between devices: 2.83 us -> 8 us  [body(): gathered = lax.all_gather(tokens, 'mp', axis=0, tiled=False)]
    slice x1 -> x0, local copies, waits for them, and re-layouts: 1.95 us -> none  [body(): gathered = lax.all_gather(tokens[skip:], 'mp', axis=0, tiled=False)]
  transfers between devices with their start and end apart: 2 -> 2, of which waited for: 2 -> 2; matrix products, arithmetic and copies ran while one was open for 0% -> 0% of each run, Pallas kernels for 8% -> 7%
where the time goes in v6:
time: 144 us
  blocking collectives  91.5 us (64%)
  waiting for transfers between devices  20.6 us (14%)
  Pallas kernels  16.7 us (12%)
  between operations  14.1 us (10%)
    all_to_all x1, blocking collectives, body(): back = lax.all_to_all(uses, 'dp', split_axis=0, concat_axis=0, tiled=True)  38.3 us
    all_to_all x1, blocking collectives, body(): got = lax.all_to_all(picked, 'dp', split_axis=0, concat_axis=0, tiled=True)  32.2 us
    all_to_all x1, blocking collectives, body(): lax.all_to_all(request, 'dp', split_axis=0, concat_axis=0, tiled=True)  21 us
    reduce_scatter x1, waiting for transfers between devices, body(): input_grad = lax.psum_scatter(terms, 'mp', scatter_dimension=1, tiled=True)  11.9 us
    all_gather x1, waiting for transfers between devices, body(): gathered = lax.all_gather(tokens, 'mp', axis=0, tiled=False)  8 us
    pallas_call x1, Pallas kernels, attend(): pl.pallas_call(kernel, out_shape=(pltpu.HBM((seq_len, mp_count * width),...  6.18 us
    pallas_call x1, Pallas kernels, sum_uses(): pl.pallas_call(kernel, out_shape=(out, out), in_specs=[SMEM, VMEM], out_s...  3.4 us
  transfers between devices with their start and end apart: 2, of which 2 were waited for; matrix products, arithmetic and copies ran while one was open for 0% of the time, Pallas kernels for 7%

profile of v6, /device:TPU:1, one launch (start us, length us, event | category | flops | bytes accessed | tf_op | source)
XLA Modules:
  0.0 144.0 jit_solution(8529985988567934137)
XLA Ops:
  7.2 0.0 copy-start
  7.2 0.0 copy-start.1
  7.2 0.0 all-gather.3.cloned.1.call-start
  7.2 0.7 all-gather.3.cloned.1.call-update
  7.9 0.0 reduce-scatter.2.cloned.1.call-start
  8.0 2.1 %request_rows.1 = (s32[64,1,128]{2,1,0:T(1,128)}, s32[32]{0:T(128)}) custom-call(s32[2,16]{1,0:T(2,128)} %bitcast.3, s32[2048]{0:T(1024)} %slot_ref.1), custom_call_target="tpu_custom_call" | custom-call | tf_op jit(solution)/shard_map/request_rows/pallas_call | solution.py:52
  10.1 21.0 %all_to_all.15.want_ref = s32[64,1,128]{2,1,0:T(1,128)} all-to-all(s32[64,1,128]{2,1,0:T(1,128)} %get-tuple-element.16), channel_id=1, replica_groups=mesh['dp'=64,'mp'=8] {'dp'}, dimensions={0} | all-to-all | bytes 65536 | tf_op jit(solution)/shard_map/all_to_all | solution.py:327
  31.1 1.4 pick_rows.1
  32.5 32.2 %all_to_all.16.got_ref = bf16[64,16,512]{2,1,0:T(8,128)(2,1)S(1)} all-to-all(bf16[64,16,512]{2,1,0:T(8,128)(2,1)S(1)} %pick_rows.1), channel_id=1, replica_groups=mesh['dp'=64,'mp'=8] {'dp'}, dimensions={0} | all-to-all | bytes 2097152 | tf_op jit(solution)/shard_map/all_to_all | solution.py:329
  64.7 0.0 copy-done
  64.7 1.1 prepare.1
  65.9 8.0 %all-gather.3.cloned.1.call-done = bf16[8192,256]{1,0:T(8,128)(2,1)} async-done(((bf16[1024,256]{1,0:T(8,128)(2,1)}), bf16[8192,256]{1,0:T(8,128)(2,1)}) %all-gather.3.cloned.1.call-update) | async-done | bytes 4194320 | tf_op jit(solution)/shard_map/all_gather | solution.py:325
  73.9 0.0 copy-done.1
  73.9 0.0 copy-start.3
  73.9 6.2 %attend.1 = (bf16[1024,2048]{1,0:T(8,128)(2,1)}, bf16[1024,256]{1,0:T(8,128)(2,1)}) custom-call(bf16[8,1024,256]{2,1,0:T(8,128)(2,1)} %bitcast.2, bf16[2048,256]{1,0:T(8,128)(2,1)S(1)} %copy-done.1, bf16[544,256]{1,0:T(8,128)(2,1)S(1)} %get-tuple-element.17.k_ref, f32[16,96,128]{2,1,0:T(8,128)S(1)} %get-tuple-element.18.pg_ref), custom_call_target="tpu_custom_call" | custom-call | tf_op jit(solution)/shard_map/attend/pallas_call | solution.py:237
  80.1 0.0 copy-start.2
  80.1 0.0 reduce-scatter.2.cloned.1.call-update
  80.1 0.0 copy-done.3
  80.1 1.0 copy-done.2
  81.1 2.5 %finish.1 = (bf16[1024,256]{1,0:T(8,128)(2,1)}, bf16[64,16,512]{2,1,0:T(8,128)(2,1)S(1)}) custom-call(s32[32]{0:T(128)S(1)} %copy-done.3, bf16[1024,256]{1,0:T(8,128)(2,1)S(1)} %copy-done.2, bf16[544,256]{1,0:T(8,128)(2,1)S(1)} %get-tuple-element.17.k_ref, bf16[544,256]{1,0:T(8,128)(2,1)S(1)} %get-tuple-element.20.v_ref, ...), custom_call_target="tpu_custom_call" | custom-call | tf_op jit(solution)/shard_map/finish/pallas_call | solution.py:299
  83.6 38.3 %all_to_all.17.back_ref = bf16[64,16,512]{2,1,0:T(8,128)(2,1)} all-to-all(bf16[64,16,512]{2,1,0:T(8,128)(2,1)S(1)} %get-tuple-element.23), channel_id=1, replica_groups=mesh['dp'=64,'mp'=8] {'dp'}, dimensions={0} | all-to-all | bytes 2097152 | tf_op jit(solution)/shard_map/all_to_all | solution.py:338
  121.8 3.4 %sum_uses.1 = (f32[32,16,256]{2,1,0:T(8,128)}, f32[32,16,256]{2,1,0:T(8,128)}) custom-call(s32[64,1,128]{2,1,0:T(1,128)} %all_to_all.15.want_ref, bf16[64,16,512]{2,1,0:T(8,128)(2,1)} %all_to_all.17.back_ref), custom_call_target="tpu_custom_call" | custom-call | tf_op jit(solution)/shard_map/sum_uses/pallas_call | solution.py:108
  125.2 11.9 %reduce-scatter.2.cloned.1.call-done = bf16[1024,256]{1,0:T(8,128)(2,1)} async-done(((bf16[1024,2048]{1,0:T(8,128)(2,1)}), bf16[1024,256]{1,0:T(8,128)(2,1)}) %reduce-scatter.2.cloned.1.call-update) | async-done | bytes 524304 | tf_op jit(solution)/shard_map/reduce_scatter | solution.py:334
Async XLA Ops:
  7.2 57.6 %copy-start = (bf16[1024,256]{1,0:T(8,128)(2,1)S(1)}, bf16[1024,256]{1,0:T(8,128)(2,1)}, u32[]{:S(2)}) copy-start(bf16[1024,256]{1,0:T(8,128)(2,1)} %cot_ref.3) | copy-start | bytes 1572868
  7.2 66.7 %copy-start.1 = (bf16[2048,256]{1,0:T(8,128)(2,1)S(1)}, bf16[2048,256]{1,0:T(8,128)(2,1)}, u32[]{:S(2)}) copy-start(bf16[2048,256]{1,0:T(8,128)(2,1)} %w_ref.1) | copy-start | bytes 3145732
  7.2 66.7 %all-gather.3.cloned.1.call-start = ((), (), s32[]{:S(2)}) async-start(), calls=%async_computation.5 | async-start | bytes 4718592 | tf_op jit(solution)/shard_map/all_gather | solution.py:325
  7.9 129.2 %reduce-scatter.2.cloned.1.call-start = ((), (), s32[]{:S(2)}) async-start(), calls=%async_computation.4 | async-start | bytes 4718592 | tf_op jit(solution)/shard_map/reduce_scatter | solution.py:334
  73.9 6.2 %copy-start.3 = (s32[32]{0:T(128)S(1)}, s32[32]{0:T(128)}, u32[]{:S(2)}) copy-start(s32[32]{0:T(128)} %get-tuple-element.15.own_ref) | copy-start | bytes 388
  80.1 1.0 copy-start.2
Sparse Core Ops, SparseCore 0:
  10.1 63.7 all-gather.2
  80.2 56.8 reduce-scatter.1

commit v7 on v6

--- a/solution.py
+++ b/solution.py
@@ -184,12 +184,12 @@
 
 
 def attend(tokens, q_weight, keys, prob_grads, seq_len, span_keys):
-    mp_count, _, width = tokens.shape
+    mp_count, given, width = tokens.shape
     heads = width // DH
     blocks = seq_len // BLOCK
     tile_keys = prob_grads.shape[1]
     scaling = 1.0 / math.sqrt(DH)
-    skip = (SPAN - 1) // 16 * 16
+    skip = seq_len - given
     half = seq_len // 2
 
     def kernel(
@@ -198,12 +198,13 @@
     ):
         def load(i):
             low, high = (half, seq_len) if i else (skip, half)
-            source = tok_hbm.at[:, low:high, :]
+            source = tok_hbm.at[:, low - skip : high - skip, :]
             return pltpu.make_async_copy(source, tok_ref.at[:, low:high, :], in_sem.at[i])
 
         def store(b):
-            rows = slice(b * BLOCK, (b + 1) * BLOCK)
-            return pltpu.make_async_copy(term_ref.at[rows, :], term_hbm.at[rows, :], out_sem.at[b])
+            low, high = max(b * BLOCK, skip), (b + 1) * BLOCK
+            target = term_hbm.at[low - skip : high - skip, :]
+            return pltpu.make_async_copy(term_ref.at[low:high, :], target, out_sem.at[b])
 
         load(0).start()
         load(1).start()
@@ -227,7 +228,7 @@
                 k = k_ref[tile_keys_of(t, span_keys), cols]
                 qg_ref[rows, cols] = (dot_tn(sg_ref[i], k) * scaling).astype(BF16)
             for b in range(low // BLOCK, (low + half) // BLOCK):
-                rows = slice(b * BLOCK, (b + 1) * BLOCK)
+                rows = slice(max(b * BLOCK, skip), (b + 1) * BLOCK)
                 term_ref[rows, :] = dot_nt(qg_ref[rows, :], w_ref[...]).astype(BF16)
                 store(b).start()
         for b in range(blocks):
@@ -237,7 +238,7 @@
     return pl.pallas_call(
         kernel,
         out_shape=(
-            pltpu.HBM((seq_len, mp_count * width), BF16),
+            pltpu.HBM((given, mp_count * width), BF16),
             pltpu.HBM((seq_len, width), BF16),
         ),
         in_specs=[HBM, VMEM, VMEM, VMEM],
@@ -322,7 +323,8 @@
     dp_count = lax.axis_size("dp")
     seq_len = tokens.shape[0]
     snip_count, nei, _ = snippet_keys.shape
-    gathered = lax.all_gather(tokens, "mp", axis=0, tiled=False)
+    skip = (SPAN - 1) // 16 * 16
+    gathered = lax.all_gather(tokens[skip:], "mp", axis=0, tiled=False)
     request, owners = request_rows(neighbour_ids.T, snippet_slot, snip_count, dp_count)
     wanted = lax.all_to_all(request, "dp", split_axis=0, concat_axis=0, tiled=True)
     picked = pick_rows(wanted, snippet_keys, snippet_values)
@@ -332,6 +334,7 @@
         gathered, q_weight, keys, prob_grads, seq_len, NEIGH * nei
     )
     input_grad = lax.psum_scatter(terms, "mp", scatter_dimension=1, tiled=True)
+    input_grad = jnp.pad(input_grad, ((skip, 0), (0, 0)))
     attended, uses = finish(
         owners, queries, keys, values, prob_grads, out_cotangent, dp_count
     )

time: 144 us -> 143 us (level)
  waiting for transfers between devices: 20.6 us -> 15.7 us
  local copies, waits for them, and re-layouts: 1.01 us -> 4.83 us
    all_gather x1, waiting for transfers between devices: 8 us -> 5.63 us  [body(): gathered = lax.all_gather(tokens[skip:], 'mp', axis=0, tiled=False)]
    slice x0 -> x1, local copies, waits for them, and re-layouts: none -> 1.95 us  [body(): gathered = lax.all_gather(tokens[skip:], 'mp', axis=0, tiled=False)]
    pad x0 -> x1, local copies, waits for them, and re-layouts: none -> 1.86 us  [body(): input_grad = jnp.pad(input_grad, ((skip, 0), (0, 0)))]
    reduce_scatter x1, waiting for transfers between devices: 11.9 us -> 10.1 us  [body(): input_grad = lax.psum_scatter(terms, 'mp', scatter_dimension=1, tiled=True)]
where the time goes in v7:
time: 143 us
  blocking collectives  91.3 us (64%)
  Pallas kernels  16.6 us (12%)
  waiting for transfers between devices  15.7 us (11%)
  between operations  14.1 us (10%)
  local copies, waits for them, and re-layouts  4.83 us (3%)
    all_to_all x1, blocking collectives, body(): back = lax.all_to_all(uses, 'dp', split_axis=0, concat_axis=0, tiled=True)  38.3 us
    all_to_all x1, blocking collectives, body(): got = lax.all_to_all(picked, 'dp', split_axis=0, concat_axis=0, tiled=True)  31.9 us
    all_to_all x1, blocking collectives, body(): lax.all_to_all(request, 'dp', split_axis=0, concat_axis=0, tiled=True)  21.2 us
    reduce_scatter x1, waiting for transfers between devices, body(): input_grad = lax.psum_scatter(terms, 'mp', scatter_dimension=1, tiled=True)  10.1 us
    pallas_call x1, Pallas kernels, attend(): pl.pallas_call(kernel, out_shape=(pltpu.HBM((given, mp_count * width), BF...  6.15 us
    all_gather x1, waiting for transfers between devices, body(): gathered = lax.all_gather(tokens[skip:], 'mp', axis=0, tiled=False)  5.63 us
    pallas_call x1, Pallas kernels, sum_uses(): pl.pallas_call(kernel, out_shape=(out, out), in_specs=[SMEM, VMEM], out_s...  3.36 us
  transfers between devices with their start and end apart: 2, of which 2 were waited for; matrix products, arithmetic and copies ran while one was open for 0% of the time, Pallas kernels for 7%

profile of v7, /device:TPU:1, one launch (start us, length us, event | category | flops | bytes accessed | tf_op | source)
XLA Modules:
  0.0 142.7 jit_solution(17910430354150072852)
XLA Ops:
  7.2 0.0 copy-start
  7.2 0.0 copy-start.1
  7.2 0.0 all-gather.3.cloned.1.call-start
  7.2 2.0 %slice.3 = bf16[976,256]{1,0:T(8,128)(2,1)} slice(bf16[1024,256]{1,0:T(8,128)(2,1)} %param.7), slice={[48:1024], [0:256]} | slice | bytes 999424 | tf_op jit(solution)/shard_map/slice | solution.py:327
  9.2 0.0 all-gather.3.cloned.1.call-update
  9.2 0.0 reduce-scatter.2.cloned.1.call-start
  9.3 2.1 %request_rows.1 = (s32[64,1,128]{2,1,0:T(1,128)}, s32[32]{0:T(128)}) custom-call(s32[2,16]{1,0:T(2,128)} %bitcast.3, s32[2048]{0:T(1024)} %slot_ref.1), custom_call_target="tpu_custom_call" | custom-call | tf_op jit(solution)/shard_map/request_rows/pallas_call | solution.py:52
  11.4 21.2 %all_to_all.15.want_ref = s32[64,1,128]{2,1,0:T(1,128)} all-to-all(s32[64,1,128]{2,1,0:T(1,128)} %get-tuple-element.16), channel_id=1, replica_groups=mesh['dp'=64,'mp'=8] {'dp'}, dimensions={0} | all-to-all | bytes 65536 | tf_op jit(solution)/shard_map/all_to_all | solution.py:329
  32.5 1.4 pick_rows.1
  33.9 31.9 %all_to_all.16.got_ref = bf16[64,16,512]{2,1,0:T(8,128)(2,1)S(1)} all-to-all(bf16[64,16,512]{2,1,0:T(8,128)(2,1)S(1)} %pick_rows.1), channel_id=1, replica_groups=mesh['dp'=64,'mp'=8] {'dp'}, dimensions={0} | all-to-all | bytes 2097152 | tf_op jit(solution)/shard_map/all_to_all | solution.py:331
  65.8 0.0 copy-done
  65.8 1.1 prepare.1
  67.0 5.6 %all-gather.3.cloned.1.call-done = bf16[7808,256]{1,0:T(8,128)(2,1)} async-done(((bf16[976,256]{1,0:T(8,128)(2,1)}), bf16[7808,256]{1,0:T(8,128)(2,1)}) %all-gather.3.cloned.1.call-update) | async-done | bytes 3997712 | tf_op jit(solution)/shard_map/all_gather | solution.py:327
  72.6 0.0 copy-done.1
  72.6 6.1 %attend.1 = (bf16[976,2048]{1,0:T(8,128)(2,1)}, bf16[1024,256]{1,0:T(8,128)(2,1)}) custom-call(bf16[8,976,256]{2,1,0:T(8,128)(2,1)} %bitcast.2, bf16[2048,256]{1,0:T(8,128)(2,1)S(1)} %copy-done.1, bf16[544,256]{1,0:T(8,128)(2,1)S(1)} %get-tuple-element.17.k_ref, f32[16,96,128]{2,1,0:T(8,128)S(1)} %get-tuple-element.18.pg_ref), custom_call_target="tpu_custom_call" | custom-call | tf_op jit(solution)/shard_map/attend/pallas_call | solution.py:238
  78.8 0.0 copy-start.2
  78.8 0.0 reduce-scatter.2.cloned.1.call-update
  78.8 0.0 copy-done.3
  78.8 1.0 copy-done.2
  79.8 2.5 %finish.1 = (bf16[1024,256]{1,0:T(8,128)(2,1)}, bf16[64,16,512]{2,1,0:T(8,128)(2,1)S(1)}) custom-call(s32[32]{0:T(128)S(1)} %copy-done.3, bf16[1024,256]{1,0:T(8,128)(2,1)S(1)} %copy-done.2, bf16[544,256]{1,0:T(8,128)(2,1)S(1)} %get-tuple-element.17.k_ref, bf16[544,256]{1,0:T(8,128)(2,1)S(1)} %get-tuple-element.20.v_ref, ...), custom_call_target="tpu_custom_call" | custom-call | tf_op jit(solution)/shard_map/finish/pallas_call | solution.py:300
  82.3 38.3 %all_to_all.17.back_ref = bf16[64,16,512]{2,1,0:T(8,128)(2,1)} all-to-all(bf16[64,16,512]{2,1,0:T(8,128)(2,1)S(1)} %get-tuple-element.23), channel_id=1, replica_groups=mesh['dp'=64,'mp'=8] {'dp'}, dimensions={0} | all-to-all | bytes 2097152 | tf_op jit(solution)/shard_map/all_to_all | solution.py:341
  120.5 3.4 %sum_uses.1 = (f32[32,16,256]{2,1,0:T(8,128)}, f32[32,16,256]{2,1,0:T(8,128)}) custom-call(s32[64,1,128]{2,1,0:T(1,128)} %all_to_all.15.want_ref, bf16[64,16,512]{2,1,0:T(8,128)(2,1)} %all_to_all.17.back_ref), custom_call_target="tpu_custom_call" | custom-call | tf_op jit(solution)/shard_map/sum_uses/pallas_call | solution.py:108
  123.9 10.1 %reduce-scatter.2.cloned.1.call-done = bf16[976,256]{1,0:T(8,128)(2,1)} async-done(((bf16[976,2048]{1,0:T(8,128)(2,1)}), bf16[976,256]{1,0:T(8,128)(2,1)}) %reduce-scatter.2.cloned.1.call-update) | async-done | bytes 499728 | tf_op jit(solution)/shard_map/reduce_scatter | solution.py:336
  134.0 1.9 %pad.4 = bf16[1024,256]{1,0:T(8,128)(2,1)} pad(bf16[976,256]{1,0:T(8,128)(2,1)} %reduce-scatter.2.cloned.1.call-done, bf16[]{:T(256)} %constant.2.clone.1), padding=48_0x0_0 | pad | bytes 1024002 | tf_op jit(solution)/shard_map/jit(_pad)/pad | solution.py:337
  (1 shorter events, 0.0 us)
Async XLA Ops:
  7.2 58.7 %copy-start = (bf16[1024,256]{1,0:T(8,128)(2,1)S(1)}, bf16[1024,256]{1,0:T(8,128)(2,1)}, u32[]{:S(2)}) copy-start(bf16[1024,256]{1,0:T(8,128)(2,1)} %cot_ref.3) | copy-start | bytes 1572868
  7.2 65.4 %copy-start.1 = (bf16[2048,256]{1,0:T(8,128)(2,1)S(1)}, bf16[2048,256]{1,0:T(8,128)(2,1)}, u32[]{:S(2)}) copy-start(bf16[2048,256]{1,0:T(8,128)(2,1)} %w_ref.1) | copy-start | bytes 3145732
  7.2 65.4 %all-gather.3.cloned.1.call-start = ((), (), s32[]{:S(2)}) async-start(), calls=%async_computation.5 | async-start | bytes 4497408 | tf_op jit(solution)/shard_map/all_gather | solution.py:327
  9.2 124.8 %reduce-scatter.2.cloned.1.call-start = ((), (), s32[]{:S(2)}) async-start(), calls=%async_computation.4 | async-start | bytes 4497408 | tf_op jit(solution)/shard_map/reduce_scatter | solution.py:336
  72.6 6.2 %copy-start.3 = (s32[32]{0:T(128)S(1)}, s32[32]{0:T(128)}, u32[]{:S(2)}) copy-start(s32[32]{0:T(128)} %get-tuple-element.15.own_ref) | copy-start | bytes 388
  78.8 1.0 copy-start.2
Sparse Core Ops, SparseCore 0:
  10.7 61.8 all-gather.2
  78.9 54.9 reduce-scatter.1

commit v8 on v6

--- a/solution.py
+++ b/solution.py
@@ -184,12 +184,12 @@
 
 
 def attend(tokens, q_weight, keys, prob_grads, seq_len, span_keys):
-    mp_count, _, width = tokens.shape
+    mp_count, given, width = tokens.shape
     heads = width // DH
     blocks = seq_len // BLOCK
     tile_keys = prob_grads.shape[1]
     scaling = 1.0 / math.sqrt(DH)
-    skip = (SPAN - 1) // 16 * 16
+    skip = seq_len - given
     half = seq_len // 2
 
     def kernel(
@@ -198,7 +198,7 @@
     ):
         def load(i):
             low, high = (half, seq_len) if i else (skip, half)
-            source = tok_hbm.at[:, low:high, :]
+            source = tok_hbm.at[:, low - skip : high - skip, :]
             return pltpu.make_async_copy(source, tok_ref.at[:, low:high, :], in_sem.at[i])
 
         def store(b):
@@ -322,7 +322,8 @@
     dp_count = lax.axis_size("dp")
     seq_len = tokens.shape[0]
     snip_count, nei, _ = snippet_keys.shape
-    gathered = lax.all_gather(tokens, "mp", axis=0, tiled=False)
+    skip = (SPAN - 1) // 16 * 16
+    gathered = lax.all_gather(tokens[skip:], "mp", axis=0, tiled=False)
     request, owners = request_rows(neighbour_ids.T, snippet_slot, snip_count, dp_count)
     wanted = lax.all_to_all(request, "dp", split_axis=0, concat_axis=0, tiled=True)
     picked = pick_rows(wanted, snippet_keys, snippet_values)

time: 144 us -> 143 us (level)
  waiting for transfers between devices: 20.6 us -> 17.4 us
  local copies, waits for them, and re-layouts: 1.01 us -> 2.97 us
    all_gather x1, waiting for transfers between devices: 8 us -> 5.48 us  [body(): gathered = lax.all_gather(tokens[skip:], 'mp', axis=0, tiled=False)]
    slice x0 -> x1, local copies, waits for them, and re-layouts: none -> 1.95 us  [body(): gathered = lax.all_gather(tokens[skip:], 'mp', axis=0, tiled=False)]
where the time goes in v8:
time: 143 us
  blocking collectives  91.5 us (64%)
  waiting for transfers between devices  17.4 us (12%)
  Pallas kernels  16.6 us (12%)
  between operations  14.1 us (10%)
  local copies, waits for them, and re-layouts  2.97 us (2%)
    all_to_all x1, blocking collectives, body(): back = lax.all_to_all(uses, 'dp', split_axis=0, concat_axis=0, tiled=True)  38.3 us
    all_to_all x1, blocking collectives, body(): got = lax.all_to_all(picked, 'dp', split_axis=0, concat_axis=0, tiled=True)  32.2 us
    all_to_all x1, blocking collectives, body(): lax.all_to_all(request, 'dp', split_axis=0, concat_axis=0, tiled=True)  21 us
    reduce_scatter x1, waiting for transfers between devices, body(): input_grad = lax.psum_scatter(terms, 'mp', scatter_dimension=1, tiled=True)  11.9 us
    pallas_call x1, Pallas kernels, attend(): pl.pallas_call(kernel, out_shape=(pltpu.HBM((seq_len, mp_count * width),...  6.18 us
    all_gather x1, waiting for transfers between devices, body(): gathered = lax.all_gather(tokens[skip:], 'mp', axis=0, tiled=False)  5.48 us
    pallas_call x1, Pallas kernels, sum_uses(): pl.pallas_call(kernel, out_shape=(out, out), in_specs=[SMEM, VMEM], out_s...  3.36 us
  transfers between devices with their start and end apart: 2, of which 2 were waited for; matrix products, arithmetic and copies ran while one was open for 0% of the time, Pallas kernels for 7%

profile of v8, /device:TPU:1, one launch (start us, length us, event | category | flops | bytes accessed | tf_op | source)
XLA Modules:
  0.0 142.7 jit_solution(5817035872000446148)
XLA Ops:
  7.2 0.0 copy-start
  7.2 0.0 copy-start.1
  7.2 0.0 all-gather.3.cloned.1.call-start
  7.2 2.0 %slice.3 = bf16[976,256]{1,0:T(8,128)(2,1)} slice(bf16[1024,256]{1,0:T(8,128)(2,1)} %param.7), slice={[48:1024], [0:256]} | slice | bytes 999424 | tf_op jit(solution)/shard_map/slice | solution.py:326
  9.2 0.0 all-gather.3.cloned.1.call-update
  9.2 0.0 reduce-scatter.2.cloned.1.call-start
  9.3 2.1 %request_rows.1 = (s32[64,1,128]{2,1,0:T(1,128)}, s32[32]{0:T(128)}) custom-call(s32[2,16]{1,0:T(2,128)} %bitcast.3, s32[2048]{0:T(1024)} %slot_ref.1), custom_call_target="tpu_custom_call" | custom-call | tf_op jit(solution)/shard_map/request_rows/pallas_call | solution.py:52
  11.4 21.0 %all_to_all.15.want_ref = s32[64,1,128]{2,1,0:T(1,128)} all-to-all(s32[64,1,128]{2,1,0:T(1,128)} %get-tuple-element.16), channel_id=1, replica_groups=mesh['dp'=64,'mp'=8] {'dp'}, dimensions={0} | all-to-all | bytes 65536 | tf_op jit(solution)/shard_map/all_to_all | solution.py:328
  32.4 1.4 pick_rows.1
  33.8 32.2 %all_to_all.16.got_ref = bf16[64,16,512]{2,1,0:T(8,128)(2,1)S(1)} all-to-all(bf16[64,16,512]{2,1,0:T(8,128)(2,1)S(1)} %pick_rows.1), channel_id=1, replica_groups=mesh['dp'=64,'mp'=8] {'dp'}, dimensions={0} | all-to-all | bytes 2097152 | tf_op jit(solution)/shard_map/all_to_all | solution.py:330
  66.0 0.0 copy-done
  66.0 1.1 prepare.1
  67.1 5.5 %all-gather.3.cloned.1.call-done = bf16[7808,256]{1,0:T(8,128)(2,1)} async-done(((bf16[976,256]{1,0:T(8,128)(2,1)}), bf16[7808,256]{1,0:T(8,128)(2,1)}) %all-gather.3.cloned.1.call-update) | async-done | bytes 3997712 | tf_op jit(solution)/shard_map/all_gather | solution.py:326
  72.6 0.0 copy-done.1
  72.6 0.0 copy-start.3
  72.6 6.2 %attend.1 = (bf16[1024,2048]{1,0:T(8,128)(2,1)}, bf16[1024,256]{1,0:T(8,128)(2,1)}) custom-call(bf16[8,976,256]{2,1,0:T(8,128)(2,1)} %bitcast.2, bf16[2048,256]{1,0:T(8,128)(2,1)S(1)} %copy-done.1, bf16[544,256]{1,0:T(8,128)(2,1)S(1)} %get-tuple-element.17.k_ref, f32[16,96,128]{2,1,0:T(8,128)S(1)} %get-tuple-element.18.pg_ref), custom_call_target="tpu_custom_call" | custom-call | tf_op jit(solution)/shard_map/attend/pallas_call | solution.py:237
  78.8 0.0 copy-start.2
  78.8 0.0 reduce-scatter.2.cloned.1.call-update
  78.8 0.0 copy-done.3
  78.8 1.0 copy-done.2
  79.8 2.5 %finish.1 = (bf16[1024,256]{1,0:T(8,128)(2,1)}, bf16[64,16,512]{2,1,0:T(8,128)(2,1)S(1)}) custom-call(s32[32]{0:T(128)S(1)} %copy-done.3, bf16[1024,256]{1,0:T(8,128)(2,1)S(1)} %copy-done.2, bf16[544,256]{1,0:T(8,128)(2,1)S(1)} %get-tuple-element.17.k_ref, bf16[544,256]{1,0:T(8,128)(2,1)S(1)} %get-tuple-element.20.v_ref, ...), custom_call_target="tpu_custom_call" | custom-call | tf_op jit(solution)/shard_map/finish/pallas_call | solution.py:299
  82.3 38.3 %all_to_all.17.back_ref = bf16[64,16,512]{2,1,0:T(8,128)(2,1)} all-to-all(bf16[64,16,512]{2,1,0:T(8,128)(2,1)S(1)} %get-tuple-element.23), channel_id=1, replica_groups=mesh['dp'=64,'mp'=8] {'dp'}, dimensions={0} | all-to-all | bytes 2097152 | tf_op jit(solution)/shard_map/all_to_all | solution.py:339
  120.6 3.4 %sum_uses.1 = (f32[32,16,256]{2,1,0:T(8,128)}, f32[32,16,256]{2,1,0:T(8,128)}) custom-call(s32[64,1,128]{2,1,0:T(1,128)} %all_to_all.15.want_ref, bf16[64,16,512]{2,1,0:T(8,128)(2,1)} %all_to_all.17.back_ref), custom_call_target="tpu_custom_call" | custom-call | tf_op jit(solution)/shard_map/sum_uses/pallas_call | solution.py:108
  123.9 11.9 %reduce-scatter.2.cloned.1.call-done = bf16[1024,256]{1,0:T(8,128)(2,1)} async-done(((bf16[1024,2048]{1,0:T(8,128)(2,1)}), bf16[1024,256]{1,0:T(8,128)(2,1)}) %reduce-scatter.2.cloned.1.call-update) | async-done | bytes 524304 | tf_op jit(solution)/shard_map/reduce_scatter | solution.py:335
Async XLA Ops:
  7.2 58.8 %copy-start = (bf16[1024,256]{1,0:T(8,128)(2,1)S(1)}, bf16[1024,256]{1,0:T(8,128)(2,1)}, u32[]{:S(2)}) copy-start(bf16[1024,256]{1,0:T(8,128)(2,1)} %cot_ref.3) | copy-start | bytes 1572868
  7.2 65.4 %copy-start.1 = (bf16[2048,256]{1,0:T(8,128)(2,1)S(1)}, bf16[2048,256]{1,0:T(8,128)(2,1)}, u32[]{:S(2)}) copy-start(bf16[2048,256]{1,0:T(8,128)(2,1)} %w_ref.1) | copy-start | bytes 3145732
  7.2 65.4 %all-gather.3.cloned.1.call-start = ((), (), s32[]{:S(2)}) async-start(), calls=%async_computation.5 | async-start | bytes 4497408 | tf_op jit(solution)/shard_map/all_gather | solution.py:326
  9.2 126.7 %reduce-scatter.2.cloned.1.call-start = ((), (), s32[]{:S(2)}) async-start(), calls=%async_computation.4 | async-start | bytes 4718592 | tf_op jit(solution)/shard_map/reduce_scatter | solution.py:335
  72.6 6.2 %copy-start.3 = (s32[32]{0:T(128)S(1)}, s32[32]{0:T(128)}, u32[]{:S(2)}) copy-start(s32[32]{0:T(128)} %get-tuple-element.15.own_ref) | copy-start | bytes 388
  78.8 1.0 copy-start.2
Sparse Core Ops, SparseCore 0:
  10.7 61.8 all-gather.2
  79.0 56.8 reduce-scatter.1
